TPU v7x, 128 devices: a whole 4x4x4 slice. The times are simulated.
128 devices in a mesh: row: 8 (over x, z_hi), col: 16 (over y, z_lo, core).
Axes of the slice: x: 4, y: 4, z: 4 (z_hi: 2, z_lo: 2; z = z_hi * 2 + z_lo), core: 2. Of those that a mesh axis runs over, the one named last changes fastest.
Arguments:
- panel_right: bfloat16 [128, 1536, 128], P('row', 'col'), may hold values from -1 to 1
- factor_inverse: bfloat16 [1536, 1536], replicated, as said below
- ranks: int32 [128], P(('row', 'col')), may hold values from 32 to 128
- owner_map: int32 [128], replicated, may hold values from 0 to 127, each once
- cores: float32 [8, 16, 16, 8, 128, 128], P('row', 'col'), may hold values from -6 to 6
Outputs:
- new_cores: float32 [8, 16, 16, 8, 128, 128], P('row', 'col')
Inputs may be any that keep to these rules, and one draw needn't show every extreme that they name: `factor_inverse`: lower triangular, the inverse of a Cholesky factor.
All inputs are finite; a program needn't handle non-finite values.
Results may differ from a plain program's by a relative error of at most 0.0033.
Values may be sent and summed in bfloat16 or wider, within the bound.
A program may use at most 128 MiB of HBM per device.

v0:
```python
import jax
import jax.numpy as jnp
from jax import lax
from jax.sharding import PartitionSpec as P


def body(panel_right, factor_inverse, ranks, owner_map, cores):
    n_row = lax.axis_size("row")
    n_col = lax.axis_size("col")
    devices = n_row * n_col
    order = factor_inverse.shape[0]
    width = panel_right.shape[2]
    whole = lax.all_to_all(panel_right, "col", split_axis=0, concat_axis=1, tiled=True)
    solved = jnp.einsum("ij,bjk->bik", factor_inverse, whole, preferred_element_type=jnp.float32)
    column = lax.broadcasted_iota(jnp.int32, (1, 1, width), 2)
    keep = column < ranks.reshape(1, 1, 1)
    panel_left = jnp.where(keep, solved, 0.0).astype(jnp.bfloat16)
    pieces = panel_left.reshape(devices, order // devices, width)
    spread = lax.all_to_all(pieces, ("row", "col"), split_axis=0, concat_axis=0, tiled=True)
    moved = jnp.take(spread, owner_map, axis=0)
    back = lax.all_to_all(moved, ("row", "col"), split_axis=0, concat_axis=0, tiled=True)
    held = back.reshape(1, order, width)
    column_set = lax.all_gather(held, "row", axis=0, tiled=True)
    gram = jnp.einsum(
        "aik,bil->abkl",
        lax.all_gather(held, "col", axis=0, tiled=True),
        column_set,
        preferred_element_type=jnp.float32,
    )
    return cores - gram[None, None]


def solution(mesh):
    return jax.shard_map(
        body,
        mesh=mesh,
        in_specs=(
            P("row", "col", None),
            P(),
            P(("row", "col")),
            P(),
            P("row", "col", None, None, None, None),
        ),
        out_specs=P("row", "col", None, None, None, None),
        check_vma=False,
    )
```

profile of v0, /device:TPU:1, one launch (start us, length us, event | category | flops | bytes accessed | tf_op | source)
XLA Modules:
  0.0 199.8 jit_solution(796832284933036660)
XLA Ops:
  6.5 0.0 copy-start
  6.5 7.5 %all-to-all-start = ((bf16[16,96,128]{2,1,0:T(8,128)(2,1)}), bf16[16,96,128]{2,1,0:T(8,128)(2,1)S(1)}, u32[]{:S(2)}, u32[]{:S(2)}) async-start(bf16[16,96,128]{2,1,0:T(8,128)(2,1)} %param.5), calls=%async_computation | async-start | bytes 786432 | tf_op jit(solution)/shard_map/all_to_all | solution.py:13
  14.7 7.9 %all-to-all-done = bf16[16,96,128]{2,1,0:T(8,128)(2,1)S(1)} async-done(((bf16[16,96,128]{2,1,0:T(8,128)(2,1)}), bf16[16,96,128]{2,1,0:T(8,128)(2,1)S(1)}, u32[]{:S(2)}, u32[]{:S(2)}) %all-to-all-start) | async-done | bytes 393248 | tf_op jit(solution)/shard_map/all_to_all | solution.py:13
  22.6 4.0 %fusion.9 = bf16[1,1536,128]{1,2,0:T(8,128)(2,1)S(1)} fusion(bf16[1536,128]{1,0:T(8,128)(2,1)S(1)} %bitcast.31, bf16[1536,1536]{1,0:T(8,128)(2,1)} %param.6, pred[128]{0:T(512)(128)(4,1)S(1)} %iota_compare_fusion), kind=kOutput, calls=%fused_computation.8 | convolution fusion | flops 604372992 | bytes 5505152 | tf_op jit(solution)/shard_map/ij,bjk->bik/dot_general | solution.py:14
  26.6 0.2 copy.14
  26.8 0.9 reshape.31
  27.7 8.2 %all-to-all-start.1 = ((bf16[128,12,128]{2,1,0:T(8,128)(2,1)}), bf16[128,12,128]{2,1,0:T(8,128)(2,1)S(1)}, u32[]{:S(2)}, u32[]{:S(2)}) async-start(bf16[128,12,128]{2,1,0:T(8,128)(2,1)} %reshape.31), calls=%async_computation.1 | async-start | bytes 1048576 | tf_op jit(solution)/shard_map/all_to_all | solution.py:19
  35.9 0.0 all-gather.3.cloned.1.call-start
  36.0 0.0 copy-done
  36.0 13.9 %all-to-all-done.1 = bf16[128,12,128]{2,1,0:T(8,128)(2,1)S(1)} async-done(((bf16[128,12,128]{2,1,0:T(8,128)(2,1)}), bf16[128,12,128]{2,1,0:T(8,128)(2,1)S(1)}, u32[]{:S(2)}, u32[]{:S(2)}) %all-to-all-start.1) | async-done | bytes 393248 | tf_op jit(solution)/shard_map/all_to_all | solution.py:19
  49.9 0.7 gather_fusion
  50.6 0.2 broadcast_select_fusion
  50.8 17.5 %all_to_all.19 = bf16[128,12,128]{2,1,0:T(8,128)(2,1)S(1)} all-to-all(bf16[128,12,128]{2,1,0:T(8,128)(2,1)S(1)} %broadcast_select_fusion), channel_id=1, replica_groups=mesh['row'=8,'col'=16] {'row','col'}, dimensions={0} | all-to-all | bytes 786432 | tf_op jit(solution)/shard_map/all_to_all | solution.py:21
  68.4 0.8 reshape.32
  69.2 0.0 all-gather.3.cloned.1.call-update
  69.2 0.0 all-gather.5.cloned.1.call-start
  69.3 0.7 all-gather.5.cloned.1.call-update
  70.0 9.2 %copy.16 = f32[1,1,16,8,128,128]{4,5,2,3,1,0:T(8,128)} copy(f32[1,1,16,8,128,128]{5,4,3,2,1,0:T(8,128)} %param.9) | data formatting | bytes 16777216 | tf_op args[4]
  79.2 48.4 %all-gather.3.cloned.1.call-done = bf16[8,1536,128]{2,1,0:T(8,128)(2,1)} async-done(((bf16[1,1536,128]{2,1,0:T(8,128)(2,1)}), bf16[8,1536,128]{2,1,0:T(8,128)(2,1)}) %all-gather.3.cloned.1.call-update) | async-done | bytes 3145744 | tf_op jit(solution)/shard_map/all_gather | solution.py:23
  127.5 43.2 %all-gather.5.cloned.1.call-done = bf16[16,1536,128]{2,1,0:T(8,128)(2,1)} async-done(((bf16[1,1536,128]{2,1,0:T(8,128)(2,1)}), bf16[16,1536,128]{2,1,0:T(8,128)(2,1)}) %all-gather.5.cloned.1.call-update) | async-done | bytes 6291472 | tf_op jit(solution)/shard_map/all_gather | solution.py:26
  170.7 13.0 %bitcast_subtract_fusion = f32[1,1,16,8,128,128]{4,5,2,3,1,0:T(8,128)} fusion(f32[1,1,16,8,128,128]{4,5,2,3,1,0:T(8,128)} %copy.16, bf16[16,1536,128]{2,1,0:T(8,128)(2,1)} %all-gather.5.cloned.1.call-done, bf16[8,1536,128]{2,1,0:T(8,128)(2,1)} %all-gather.3.cloned.1.call-done), kind=kOutput, calls=%fused_computation.1 | convolution fusion | flops 6444548096 | bytes 26214400 | tf_op jit(solution)/shard_map/aik,bil->abkl/dot_general | solution.py:24
  183.7 9.3 %copy.17 = f32[1,1,16,8,128,128]{5,4,3,2,1,0:T(8,128)} copy(f32[1,1,16,8,128,128]{4,5,2,3,1,0:T(8,128)} %bitcast_subtract_fusion) | data formatting | bytes 16777216 | tf_op jit(solution)/shard_map/sub | solution.py:30
  (4 shorter events, 0.0 us)
Async XLA Ops:
  6.5 29.4 %copy-start = (s32[128]{0:T(128)S(1)}, s32[128]{0:T(128)}, u32[]{:S(2)}) copy-start(s32[128]{0:T(128)} %param.8) | copy-start | bytes 1540
  6.5 16.1 %all-to-all-start = ((bf16[16,96,128]{2,1,0:T(8,128)(2,1)}), bf16[16,96,128]{2,1,0:T(8,128)(2,1)S(1)}, u32[]{:S(2)}, u32[]{:S(2)}) async-start(bf16[16,96,128]{2,1,0:T(8,128)(2,1)} %param.5), calls=%async_computation | async-start | bytes 786432 | tf_op jit(solution)/shard_map/all_to_all | solution.py:13
  27.7 22.2 %all-to-all-start.1 = ((bf16[128,12,128]{2,1,0:T(8,128)(2,1)}), bf16[128,12,128]{2,1,0:T(8,128)(2,1)S(1)}, u32[]{:S(2)}, u32[]{:S(2)}) async-start(bf16[128,12,128]{2,1,0:T(8,128)(2,1)} %reshape.31), calls=%async_computation.1 | async-start | bytes 1048576 | tf_op jit(solution)/shard_map/all_to_all | solution.py:19
  35.9 91.6 %all-gather.3.cloned.1.call-start = ((), (), s32[]{:S(2)}) async-start(), calls=%async_computation.3 | async-start | bytes 3538944 | tf_op jit(solution)/shard_map/all_gather | solution.py:23
  69.2 101.5 %all-gather.5.cloned.1.call-start = ((), (), s32[]{:S(2)}) async-start(), calls=%async_computation.4 | async-start | bytes 6684672 | tf_op jit(solution)/shard_map/all_gather | solution.py:26
Sparse Core Ops, SparseCore 0:
  69.4 58.1 all-gather.2
  129.2 41.4 all-gather.4
where the time goes:
time: 200 us
  waiting for transfers between devices  114 us (57%)
  local copies, waits for them, and re-layouts  21.1 us (11%)
  blocking collectives  17.5 us (9%)
  matrix products  17 us (8%)
  starting transfers between devices  15.7 us (8%)
  between operations  14.1 us (7%)
    all_gather x1, waiting for transfers between devices, body(): column_set = lax.all_gather(held, 'row', axis=0, tiled=True)  48.4 us
    all_gather x1, waiting for transfers between devices, body(): lax.all_gather(held, 'col', axis=0, tiled=True)  43.2 us
    all_to_all x1, blocking collectives, body(): lax.all_to_all(moved, ('row', 'col'), split_axis=0, concat_axis=0, tiled=...  17.5 us
    all_to_all x1, waiting for transfers between devices, body(): lax.all_to_all(pieces, ('row', 'col'), split_axis=0, concat_axis=0, tiled...  13.9 us
    dot_general x1, matrix products, body(): jnp.einsum('aik,bil->abkl', lax.all_gather(held, 'col', axis=0, tiled=Tru...  13 us
    sub x1, local copies, waits for them, and re-layouts, body(): return cores - gram[None, None]  9.25 us
    unnamed x3, local copies, waits for them, and re-layouts  9.17 us
    all_to_all x1, starting transfers between devices, body(): lax.all_to_all(pieces, ('row', 'col'), split_axis=0, concat_axis=0, tiled...  8.18 us
  transfers between devices with their start and end apart: 4, of which 4 were waited for; matrix products, arithmetic and copies ran while one was open for 5% of the time, Pallas kernels for 0%

commit v1 on v0

v1 whole, which is shorter than its diff:
```python
import jax
import jax.numpy as jnp
from jax import lax
from jax.experimental import pallas as pl
from jax.experimental.pallas import tpu as pltpu
from jax.sharding import PartitionSpec as P

B = 1536
R = 128
NP = 128
N_ROW = 8
N_COL = 16
ROWS = B // N_COL
PART = 16
PARTS = ROWS // PART
HB = B // 2
HR = R // 2
MESH = pl.DeviceIdType.MESH


def kernel(owner_ref, rank_ref, panel_hbm, inverse_hbm, cores_hbm, out_ref,
           spread, moved, held_rows, held, inverse, rank_mine, rank_rows, rank_pack, rank_all,
           right, left, send_sem, local_sem, sem_spread, sem_rank_a, sem_rank_b, sem_back, sem_rows,
           sem_right, sem_left):
    r = lax.axis_index("row")
    c = lax.axis_index("col")
    x, zh = r // 2, r % 2
    y, zl, h = c // 4, (c // 2) % 2, c % 2

    inverse_copy = pltpu.make_async_copy(inverse_hbm, inverse, local_sem.at[0])
    inverse_copy.start()
    cores_copy = pltpu.make_async_copy(cores_hbm, out_ref, local_sem.at[1])
    cores_copy.start()

    barrier = pltpu.get_barrier_semaphore()
    for d in range(1, N_ROW):
        pl.semaphore_signal(barrier, inc=1, device_id={"row": (r + d) % N_ROW, "col": c}, device_id_type=MESH)
    for d in range(1, N_COL):
        pl.semaphore_signal(barrier, inc=1, device_id={"row": r, "col": (c + d) % N_COL}, device_id_type=MESH)
    pl.semaphore_wait(barrier, N_ROW + N_COL - 2)

    sends = []
    counter = [0]

    def send(src, dst, recv, row, col, when=None):
        desc = pltpu.make_async_remote_copy(
            src_ref=src, dst_ref=dst, send_sem=send_sem.at[counter[0]], recv_sem=recv,
            device_id={"row": row, "col": col}, device_id_type=MESH)
        counter[0] += 1
        if when is None:
            desc.start()
        else:
            pl.when(when)(desc.start)
        sends.append((desc, when))

    def arrived(dst, recv):
        pltpu.make_async_remote_copy(
            src_ref=dst, dst_ref=dst, send_sem=recv, recv_sem=recv,
            device_id={"row": r, "col": c}, device_id_type=MESH).wait_recv()

    my_part = (r - c - 1) % N_ROW
    active = my_part < PARTS
    for d in range(1, N_ROW):
        to = (r + d) % N_ROW
        part = (to - c - 1) % N_ROW
        send(panel_hbm.at[:, pl.ds(pl.multiple_of(jnp.minimum(part, PARTS - 1) * PART, PART), PART), :],
             spread.at[pl.ds(r * N_COL, N_COL)], sem_spread.at[r], to, c, part < PARTS)
    own_part = pl.ds(pl.multiple_of(jnp.minimum(my_part, PARTS - 1) * PART, PART), PART)
    own_spread = pltpu.make_async_copy(
        panel_hbm.at[:, own_part, :], spread.at[pl.ds(r * N_COL, N_COL)], local_sem.at[2])
    pl.when(active)(own_spread.start)

    rank_mine[...] = jnp.full((8, R), rank_ref[0], jnp.int32)
    for d in range(1, N_ROW):
        send(rank_mine, rank_rows.at[r], sem_rank_a.at[r], (r + d) % N_ROW, c)
    rank_rows[r] = rank_mine[...]

    @pl.when(active)
    def _():
        own_spread.wait()
        for d in range(1, N_ROW):
            frm = (r + d) % N_ROW
            arrived(spread.at[pl.ds(frm * N_COL, N_COL)], sem_spread.at[frm])

        @pl.loop(0, NP, unroll=8)
        def _(p):
            moved[p] = spread[owner_ref[p]]

    for d in range(1, N_ROW):
        to = (r + d) % N_ROW
        send(moved.at[pl.ds(to * N_COL, N_COL)], held_rows.at[:, own_part, :],
             sem_back.at[my_part], to, c, active)
    own_back = pltpu.make_async_copy(
        moved.at[pl.ds(r * N_COL, N_COL)], held_rows.at[:, own_part, :], local_sem.at[2])
    pl.when(active)(own_back.start)

    for d in range(1, N_ROW):
        frm = (r + d) % N_ROW
        arrived(rank_rows.at[frm], sem_rank_a.at[frm])
    for k in range(N_ROW):
        rank_pack[pl.ds(k, 1), :] = rank_rows[k, pl.ds(0, 1), :]
    for d in range(1, N_COL):
        send(rank_pack, rank_all.at[c], sem_rank_b.at[c], r, (c + d) % N_COL)
    rank_all[c] = rank_pack[...]

    pl.when(active)(own_back.wait)
    for part in range(PARTS):
        frm = (part + c + 1) % N_ROW

        @pl.when(frm != r)
        def _(part=part):
            arrived(held_rows.at[:, pl.ds(part * PART, PART), :], sem_back.at[part])

    for d in range(1, N_COL):
        to = (c + d) % N_COL
        send(held_rows.at[to], held.at[pl.ds(pl.multiple_of(c * ROWS, 16), ROWS), :], sem_rows.at[c], r, to)
    own_rows = pltpu.make_async_copy(
        held_rows.at[c], held.at[pl.ds(pl.multiple_of(c * ROWS, 16), ROWS), :], local_sem.at[2])
    own_rows.start()
    for d in range(1, N_COL):
        frm = (c + d) % N_COL
        arrived(rank_all.at[frm], sem_rank_b.at[frm])
    inverse_copy.wait()
    own_rows.wait()
    for d in range(1, N_COL):
        frm = (c + d) % N_COL
        arrived(held.at[pl.ds(pl.multiple_of(frm * ROWS, 16), ROWS), :], sem_rows.at[frm])

    block = owner_ref[r * N_COL + c]
    rank = rank_all[block % N_COL, pl.ds(block // N_COL, 1), :]
    keep = lax.broadcasted_iota(jnp.int32, (1, R), 1) < rank
    step = 256
    for i in range(B // step):
        rows = slice(i * step, (i + 1) * step)
        done = (i + 1) * step
        solved = jnp.dot(inverse[rows, :done], held[:done, :], preferred_element_type=jnp.float32)
        solved = jnp.where(keep, solved, 0.0)
        right[r, rows, :] = solved.astype(jnp.bfloat16)
        left[c, :, rows] = solved.T.astype(jnp.bfloat16)

    def row_of(dx, flip):
        return ((x + dx) % 4) * 2 + (1 - zh if flip else zh)

    def col_of(dy, flip, other=0):
        return ((y + dy) % 4) * 4 + (1 - zl if flip else zl) * 2 + (1 - h if other else h)

    sibling = col_of(0, 0, 1)

    def send_right(slot, dx, flip, part=None):
        if part is None:
            ref, sem = right.at[slot], sem_right.at[slot, 0]
        else:
            ref, sem = right.at[slot, pl.ds(part * HB, HB), :], sem_right.at[slot, part]
        send(ref, ref, sem, row_of(dx, flip), c)

    def send_left(slot, to, part=None):
        if part is None:
            ref, sem = left.at[slot], sem_left.at[slot, 0]
        else:
            ref, sem = left.at[slot, pl.ds(part * HR, HR), :], sem_left.at[slot, part]
        send(ref, ref, sem, r, to)

    def wait_right(slot):
        arrived(right.at[slot], sem_right.at[slot, 0])

    def wait_left(slot):
        arrived(left.at[slot], sem_left.at[slot, 0])

    def wait_halves(ref, sem, slot, half):
        for part in range(2):
            arrived(ref.at[slot, pl.ds(part * half, half), :], sem.at[slot, part])

    def gram(pairs, first, second):
        for pair in pairs:
            lhs = left[pl.ds(pair * 2, 2)].reshape(2 * R, B)
            rhs = jnp.concatenate([right[first], right[second]], axis=1)
            g = jnp.dot(lhs, rhs, preferred_element_type=jnp.float32)
            for i in range(2):
                for j, slot in enumerate((first, second)):
                    out_ref[pair * 2 + i, slot] -= g[i * R:(i + 1) * R, j * R:(j + 1) * R]

    def pair_of(dy, flip):
        return ((y + dy) % 4) * 2 + (1 - zl if flip else zl)

    def gram_set(pairs, rights):
        for first, second in rights:
            gram(pairs, first, second)

    own_pair = (row_of(0, 0), row_of(0, 1))
    near_o = (row_of(-1, 0), row_of(1, 0))
    near_q = (row_of(-1, 1), row_of(1, 1))
    far = (row_of(2, 0), row_of(2, 1))

    for dx in (1, -1):
        send_right(r, dx, 0)
    send_right(r, 0, 1)
    for dy in (1, -1):
        send_left(c, col_of(dy, 0))
    send_left(c, col_of(0, 1))
    send_left(c, sibling)

    wait_right(row_of(0, 1))
    for dx in (1, -1):
        send_right(row_of(0, 1), dx, 0)
    wait_left(col_of(0, 1))
    for dy in (1, -1):
        send_left(col_of(0, 1), col_of(dy, 0))
    send_left(col_of(0, 1), sibling)

    cores_copy.wait()
    wait_left(col_of(0, 0, 1))
    gram_set([pair_of(0, 0)], [own_pair])

    for part, d in ((0, -1), (1, 1)):
        wait_right(row_of(d, 0))
        send_right(row_of(d, 0), -d, 0, part)
    for part, d in ((0, -1), (1, 1)):
        wait_left(col_of(d, 0))
        send_left(col_of(d, 0), col_of(-d, 0), part)
        send_left(col_of(d, 0), sibling)

    wait_left(col_of(0, 1, 1))
    gram_set([pair_of(0, 0)], [near_o])
    gram_set([pair_of(0, 1)], [own_pair, near_o])
    wait_halves(right, sem_right, row_of(2, 0), HB)
    wait_halves(left, sem_left, col_of(2, 0), HR)
    send_left(col_of(2, 0), sibling)
    for d in (-1, 1):
        wait_left(col_of(d, 0, 1))
        gram_set([pair_of(d, 0)], [own_pair, near_o])

    for part, d in ((0, -1), (1, 1)):
        wait_right(row_of(d, 1))
        send_right(row_of(d, 1), -d, 0, part)
    for part, d in ((0, -1), (1, 1)):
        wait_left(col_of(d, 1))
        send_left(col_of(d, 1), col_of(-d, 0), part)
        send_left(col_of(d, 1), sibling)
    wait_left(col_of(2, 0, 1))
    gram_set([pair_of(2, 0)], [own_pair, near_o, near_q])
    gram_set([pair_of(0, 0), pair_of(0, 1), pair_of(-1, 0), pair_of(1, 0)], [near_q])
    for d in (-1, 1):
        wait_left(col_of(d, 1, 1))
        gram_set([pair_of(d, 1)], [own_pair, near_o, near_q])

    wait_halves(left, sem_left, col_of(2, 1), HR)
    send_left(col_of(2, 1), sibling)
    wait_halves(right, sem_right, row_of(2, 1), HB)
    gram_set([pair_of(0, 0), pair_of(0, 1), pair_of(-1, 0), pair_of(1, 0), pair_of(2, 0),
              pair_of(-1, 1), pair_of(1, 1)], [far])
    wait_left(col_of(2, 1, 1))
    gram_set([pair_of(2, 1)], [own_pair, near_o, near_q, far])

    for desc, when in sends:
        if when is None:
            desc.wait_send()
        else:
            pl.when(when)(desc.wait_send)


def body(panel_right, factor_inverse, ranks, owner_map, cores):
    grams = 16 * 8 * 128 * 128
    vmem = pl.BlockSpec(memory_space=pltpu.VMEM)
    smem = pl.BlockSpec(memory_space=pltpu.SMEM)
    anywhere = pl.BlockSpec(memory_space=pl.ANY)
    bf16 = jnp.bfloat16
    dma = pltpu.SemaphoreType.DMA
    out = pl.pallas_call(
        kernel,
        out_shape=jax.ShapeDtypeStruct((N_COL, N_ROW, R, R), jnp.float32),
        in_specs=[smem, smem, anywhere, anywhere, anywhere],
        out_specs=vmem,
        scratch_shapes=[
            pltpu.VMEM((NP, PART, R), bf16),
            pltpu.VMEM((NP, PART, R), bf16),
            pltpu.VMEM((N_COL, ROWS, R), bf16),
            pltpu.VMEM((B, R), bf16),
            pltpu.VMEM((B, B), bf16),
            pltpu.VMEM((8, R), jnp.int32),
            pltpu.VMEM((N_ROW, 8, R), jnp.int32),
            pltpu.VMEM((8, R), jnp.int32),
            pltpu.VMEM((N_COL, 8, R), jnp.int32),
            pltpu.VMEM((N_ROW, B, R), bf16),
            pltpu.VMEM((N_COL, R, B), bf16),
            dma((96,)),
            dma((3,)),
            dma((N_ROW,)),
            dma((N_ROW,)),
            dma((N_COL,)),
            dma((N_ROW,)),
            dma((N_COL,)),
            dma((N_ROW, 2)),
            dma((N_COL, 2)),
        ],
        compiler_params=pltpu.CompilerParams(
            collective_id=0, has_side_effects=True, vmem_limit_bytes=48 << 20),
        cost_estimate=pl.CostEstimate(
            flops=2 * grams * B, bytes_accessed=4 * grams * 2, transcendentals=0),
    )(owner_map, ranks, panel_right, factor_inverse, cores.reshape(N_COL, N_ROW, R, R))
    return out.reshape(cores.shape)


def solution(mesh):
    return jax.shard_map(
        body,
        mesh=mesh,
        in_specs=(
            P("row", "col", None),
            P(),
            P(("row", "col")),
            P(),
            P("row", "col", None, None, None, None),
        ),
        out_specs=P("row", "col", None, None, None, None),
        check_vma=False,
    )
```

time: 200 us -> 94.2 us (0.47)
  waiting for transfers between devices: 114 us -> 0 us
  Pallas kernels: 0 us -> 81.5 us
  blocking collectives: 17.5 us -> 0 us
  matrix products: 17 us -> 0 us
  starting transfers between devices: 15.7 us -> 0 us
  between operations: 14.1 us -> 0.67 us
  local copies, waits for them, and re-layouts: 21.1 us -> 11.9 us
    all_gather x2 -> x0, waiting for transfers between devices: 91.6 us -> none  [the longest x1 48.4 us: body(): column_set = lax.all_gather(held, 'row', axis=0, tiled=True)]
    pallas_call x0 -> x1, Pallas kernels: none -> 81.5 us  [body(): pl.pallas_call(kernel, out_shape=jax.ShapeDtypeStruct((N_COL, N_ROW, R, R...]
    all_to_all x2 -> x0, waiting for transfers between devices: 21.8 us -> none  [the longest x1 13.9 us: body(): lax.all_to_all(pieces, ('row', 'col'), split_axis=0, concat_axis=0, tiled...]
    all_to_all x1 -> x0, blocking collectives: 17.5 us -> none  [body(): lax.all_to_all(moved, ('row', 'col'), split_axis=0, concat_axis=0, tiled=...]
    dot_general x2 -> x0, matrix products: 17 us -> none  [the longest x1 13 us: body(): jnp.einsum('aik,bil->abkl', lax.all_gather(held, 'col', axis=0, tiled=Tru...]
    all_to_all x2 -> x0, starting transfers between devices: 15.6 us -> none  [the longest x1 8.18 us: body(): lax.all_to_all(pieces, ('row', 'col'), split_axis=0, concat_axis=0, tiled...]
    sub x1 -> x0, local copies, waits for them, and re-layouts: 9.25 us -> none  [body(): return cores - gram[None, None]]
    unnamed x3 -> x7, local copies, waits for them, and re-layouts: 9.17 us -> 11.9 us
  transfers between devices with their start and end apart: 4 -> 0, of which waited for: 4 -> 0; matrix products, arithmetic and copies ran while one was open for 5% -> 0% of each run, Pallas kernels for 0% -> 0%
where the time goes in v1:
time: 94.2 us; the launch traced here: 94 us
  Pallas kernels  81.5 us (87%)
  local copies, waits for them, and re-layouts  11.9 us (13%)
    pallas_call x1, Pallas kernels, body(): pl.pallas_call(kernel, out_shape=jax.ShapeDtypeStruct((N_COL, N_ROW, R, R...  81.5 us
    unnamed x7, local copies, waits for them, and re-layouts  11.9 us

profile of v1, /device:TPU:1, one launch (start us, length us, event | category | flops | bytes accessed | tf_op | source)
XLA Modules:
  0.0 94.0 jit_solution(3767457832162561060)
XLA Ops:
  0.7 0.0 copy-start
  0.7 2.3 %copy-done = bf16[1536,1536]{1,0:T(8,128)(2,1)S(1)} copy-done((bf16[1536,1536]{1,0:T(8,128)(2,1)S(1)}, bf16[1536,1536]{1,0:T(8,128)(2,1)}, u32[]{:S(2)}) %copy-start) | copy-done | bytes 4718616
  3.0 0.0 copy-start.1
  3.0 1.0 %copy-done.1 = bf16[16,96,128]{2,1,0:T(8,128)(2,1)S(1)} copy-done((bf16[16,96,128]{2,1,0:T(8,128)(2,1)S(1)}, bf16[16,96,128]{2,1,0:T(8,128)(2,1)}, u32[]{:S(2)}) %copy-start.1) | copy-done | bytes 393240
  4.0 0.0 copy-start.2
  4.0 0.7 copy-done.2
  4.6 81.5 %shard_map.55 = f32[16,8,128,128]{3,2,1,0:T(8,128)} custom-call(s32[128]{0:T(128)S(1)} %copy-done.2, s32[1]{0:T(128)S(6)} %copy.7.rank_ref, bf16[16,96,128]{2,1,0:T(8,128)(2,1)S(1)} %copy-done.1, bf16[1536,1536]{1,0:T(8,128)(2,1)S(1)} %copy-done, f32[16,8,128,128]{3,2,1,0:T(8,128)} %bitcast.3), custom_call_target="tpu_custom_call" | custom-call | flops 6442450944 | bytes 16777216 | tf_op jit(solution)/shard_map/pallas_call | solution.py:268
  86.1 7.9 %copy.8 = f32[1,1,16,8,128,128]{5,4,3,2,1,0:T(8,128)} copy(f32[1,1,16,8,128,128]{5,4,3,2,1,0:T(8,128)} %bitcast.2) | data formatting | bytes 16777216
Async XLA Ops:
  0.7 2.3 %copy-start = (bf16[1536,1536]{1,0:T(8,128)(2,1)S(1)}, bf16[1536,1536]{1,0:T(8,128)(2,1)}, u32[]{:S(2)}) copy-start(bf16[1536,1536]{1,0:T(8,128)(2,1)} %inverse_hbm.1) | copy-start | bytes 14155780
  3.0 1.0 %copy-start.1 = (bf16[16,96,128]{2,1,0:T(8,128)(2,1)S(1)}, bf16[16,96,128]{2,1,0:T(8,128)(2,1)}, u32[]{:S(2)}) copy-start(bf16[16,96,128]{2,1,0:T(8,128)(2,1)} %panel_hbm.1) | copy-start | bytes 1179652
  4.0 0.7 copy-start.2

commit v2 on v1

--- a/solution.py
+++ b/solution.py
@@ -146,110 +146,132 @@
 
     sibling = col_of(0, 0, 1)
 
-    def send_right(slot, dx, flip, part=None):
-        if part is None:
-            ref, sem = right.at[slot], sem_right.at[slot, 0]
-        else:
-            ref, sem = right.at[slot, pl.ds(part * HB, HB), :], sem_right.at[slot, part]
-        send(ref, ref, sem, row_of(dx, flip), c)
-
-    def send_left(slot, to, part=None):
-        if part is None:
-            ref, sem = left.at[slot], sem_left.at[slot, 0]
-        else:
-            ref, sem = left.at[slot, pl.ds(part * HR, HR), :], sem_left.at[slot, part]
-        send(ref, ref, sem, r, to)
-
-    def wait_right(slot):
-        arrived(right.at[slot], sem_right.at[slot, 0])
-
-    def wait_left(slot):
+    def half(ref, slot, part):
+        size = HB if ref is right else HR
+        return ref.at[slot, pl.ds(part * size, size), :]
+
+    def send_right(slot, part, dx, flip=0):
+        ref = half(right, slot, part)
+        send(ref, ref, sem_right.at[slot, part], row_of(dx, flip), c)
+
+    def send_left(slot, part, dy, flip=0):
+        ref = half(left, slot, part)
+        send(ref, ref, sem_left.at[slot, part], r, col_of(dy, flip))
+
+    def share(slot):
+        send(left.at[slot], left.at[slot], sem_left.at[slot, 0], r, sibling)
+
+    def wait_right(slot, part):
+        arrived(half(right, slot, part), sem_right.at[slot, part])
+
+    def wait_left(slot, part):
+        arrived(half(left, slot, part), sem_left.at[slot, part])
+
+    def wait_shared(slot):
         arrived(left.at[slot], sem_left.at[slot, 0])
 
-    def wait_halves(ref, sem, slot, half):
-        for part in range(2):
-            arrived(ref.at[slot, pl.ds(part * half, half), :], sem.at[slot, part])
-
-    def gram(pairs, first, second):
-        for pair in pairs:
-            lhs = left[pl.ds(pair * 2, 2)].reshape(2 * R, B)
-            rhs = jnp.concatenate([right[first], right[second]], axis=1)
-            g = jnp.dot(lhs, rhs, preferred_element_type=jnp.float32)
-            for i in range(2):
-                for j, slot in enumerate((first, second)):
-                    out_ref[pair * 2 + i, slot] -= g[i * R:(i + 1) * R, j * R:(j + 1) * R]
+    def gram(pair, first, second):
+        lhs = left[pl.ds(pair * 2, 2)].reshape(2 * R, B)
+        rhs = jnp.concatenate([right[first], right[second]], axis=1)
+        g = jnp.dot(lhs, rhs, preferred_element_type=jnp.float32)
+        for i in range(2):
+            for j, slot in enumerate((first, second)):
+                out_ref[pair * 2 + i, slot] -= g[i * R:(i + 1) * R, j * R:(j + 1) * R]
 
     def pair_of(dy, flip):
         return ((y + dy) % 4) * 2 + (1 - zl if flip else zl)
 
-    def gram_set(pairs, rights):
-        for first, second in rights:
-            gram(pairs, first, second)
-
-    own_pair = (row_of(0, 0), row_of(0, 1))
     near_o = (row_of(-1, 0), row_of(1, 0))
+    own_far = (row_of(0, 0), row_of(2, 0))
     near_q = (row_of(-1, 1), row_of(1, 1))
-    far = (row_of(2, 0), row_of(2, 1))
-
-    for dx in (1, -1):
-        send_right(r, dx, 0)
-    send_right(r, 0, 1)
-    for dy in (1, -1):
-        send_left(c, col_of(dy, 0))
-    send_left(c, col_of(0, 1))
-    send_left(c, sibling)
-
-    wait_right(row_of(0, 1))
-    for dx in (1, -1):
-        send_right(row_of(0, 1), dx, 0)
-    wait_left(col_of(0, 1))
-    for dy in (1, -1):
-        send_left(col_of(0, 1), col_of(dy, 0))
-    send_left(col_of(0, 1), sibling)
-
+    flip_far = (row_of(0, 1), row_of(2, 1))
+    r_q, c_q = row_of(0, 1), col_of(0, 1)
+    toward = ((0, 1), (1, -1))
+
+    send_left(c, 0, 0, 1)
+    send_right(r, 0, 0, 1)
+    for part, d in toward:
+        send_right(r, part, d)
+        send_left(c, part, d)
+    for part, d in toward:
+        send_right(r, 1 - part, d)
+        send_left(c, 1 - part, d)
+    send_left(c, 1, 0, 1)
+    send_right(r, 1, 0, 1)
+    share(c)
+
+    for part, d in toward:
+        wait_right(row_of(-d, 0), part)
+        send_right(row_of(-d, 0), part, d)
+        wait_left(col_of(-d, 0), part)
+        send_left(col_of(-d, 0), part, d)
+    wait_left(c_q, 0)
+    for d in (1, -1):
+        send_left(c_q, 0, d)
+    wait_right(r_q, 0)
+    for d in (1, -1):
+        send_right(r_q, 0, d)
     cores_copy.wait()
-    wait_left(col_of(0, 0, 1))
-    gram_set([pair_of(0, 0)], [own_pair])
-
-    for part, d in ((0, -1), (1, 1)):
-        wait_right(row_of(d, 0))
-        send_right(row_of(d, 0), -d, 0, part)
-    for part, d in ((0, -1), (1, 1)):
-        wait_left(col_of(d, 0))
-        send_left(col_of(d, 0), col_of(-d, 0), part)
-        send_left(col_of(d, 0), sibling)
-
-    wait_left(col_of(0, 1, 1))
-    gram_set([pair_of(0, 0)], [near_o])
-    gram_set([pair_of(0, 1)], [own_pair, near_o])
-    wait_halves(right, sem_right, row_of(2, 0), HB)
-    wait_halves(left, sem_left, col_of(2, 0), HR)
-    send_left(col_of(2, 0), sibling)
+    wait_shared(col_of(0, 0, 1))
+
+    for part, d in toward:
+        wait_right(row_of(-d, 0), 1 - part)
+        wait_left(col_of(-d, 0), 1 - part)
+        share(col_of(-d, 0))
+    gram(pair_of(0, 0), *near_o)
+
+    wait_left(c_q, 1)
+    for d in (1, -1):
+        send_left(c_q, 1, d)
+    share(c_q)
+    for part in range(2):
+        wait_right(row_of(2, 0), part)
+        wait_left(col_of(2, 0), part)
+    share(col_of(2, 0))
     for d in (-1, 1):
-        wait_left(col_of(d, 0, 1))
-        gram_set([pair_of(d, 0)], [own_pair, near_o])
-
-    for part, d in ((0, -1), (1, 1)):
-        wait_right(row_of(d, 1))
-        send_right(row_of(d, 1), -d, 0, part)
-    for part, d in ((0, -1), (1, 1)):
-        wait_left(col_of(d, 1))
-        send_left(col_of(d, 1), col_of(-d, 0), part)
-        send_left(col_of(d, 1), sibling)
-    wait_left(col_of(2, 0, 1))
-    gram_set([pair_of(2, 0)], [own_pair, near_o, near_q])
-    gram_set([pair_of(0, 0), pair_of(0, 1), pair_of(-1, 0), pair_of(1, 0)], [near_q])
+        wait_shared(col_of(d, 0, 1))
+        gram(pair_of(d, 0), *near_o)
+    wait_right(r_q, 1)
+    for d in (1, -1):
+        send_right(r_q, 1, d)
+
+    wait_shared(col_of(0, 1, 1))
+    gram(pair_of(0, 1), *near_o)
+    gram(pair_of(0, 1), *own_far)
+    gram(pair_of(0, 0), *own_far)
+    for part, d in toward:
+        wait_left(col_of(-d, 1), part)
+        send_left(col_of(-d, 1), part, d)
+    wait_shared(col_of(2, 0, 1))
+    gram(pair_of(2, 0), *near_o)
+    gram(pair_of(2, 0), *own_far)
+    for part, d in toward:
+        wait_right(row_of(-d, 1), part)
+        send_right(row_of(-d, 1), part, d)
     for d in (-1, 1):
-        wait_left(col_of(d, 1, 1))
-        gram_set([pair_of(d, 1)], [own_pair, near_o, near_q])
-
-    wait_halves(left, sem_left, col_of(2, 1), HR)
-    send_left(col_of(2, 1), sibling)
-    wait_halves(right, sem_right, row_of(2, 1), HB)
-    gram_set([pair_of(0, 0), pair_of(0, 1), pair_of(-1, 0), pair_of(1, 0), pair_of(2, 0),
-              pair_of(-1, 1), pair_of(1, 1)], [far])
-    wait_left(col_of(2, 1, 1))
-    gram_set([pair_of(2, 1)], [own_pair, near_o, near_q, far])
+        gram(pair_of(d, 0), *own_far)
+    for part, d in toward:
+        wait_left(col_of(-d, 1), 1 - part)
+        share(col_of(-d, 1))
+    for d in (-1, 1):
+        wait_shared(col_of(d, 1, 1))
+        gram(pair_of(d, 1), *near_o)
+        gram(pair_of(d, 1), *own_far)
+    for part, d in toward:
+        wait_right(row_of(-d, 1), 1 - part)
+    for pair in (pair_of(0, 0), pair_of(0, 1), pair_of(2, 0), pair_of(-1, 0), pair_of(1, 0), pair_of(-1, 1), pair_of(1, 1)):
+        gram(pair, *near_q)
+
+    for part in range(2):
+        wait_left(col_of(2, 1), part)
+    share(col_of(2, 1))
+    for part in range(2):
+        wait_right(row_of(2, 1), part)
+    for pair in (pair_of(0, 0), pair_of(0, 1), pair_of(2, 0), pair_of(-1, 0), pair_of(1, 0), pair_of(-1, 1), pair_of(1, 1)):
+        gram(pair, *flip_far)
+    wait_shared(col_of(2, 1, 1))
+    for rights in (near_o, own_far, near_q, flip_far):
+        gram(pair_of(2, 1), *rights)
 
     for desc, when in sends:
         if when is None:
@@ -262,13 +284,13 @@
     grams = 16 * 8 * 128 * 128
     vmem = pl.BlockSpec(memory_space=pltpu.VMEM)
     smem = pl.BlockSpec(memory_space=pltpu.SMEM)
-    anywhere = pl.BlockSpec(memory_space=pl.ANY)
+    hbm = pl.BlockSpec(memory_space=pltpu.HBM)
     bf16 = jnp.bfloat16
     dma = pltpu.SemaphoreType.DMA
     out = pl.pallas_call(
         kernel,
-        out_shape=jax.ShapeDtypeStruct((N_COL, N_ROW, R, R), jnp.float32),
-        in_specs=[smem, smem, anywhere, anywhere, anywhere],
+        out_shape=pltpu.VMEM((N_COL, N_ROW, R, R), jnp.float32),
+        in_specs=[smem, smem, hbm, hbm, hbm],
         out_specs=vmem,
         scratch_shapes=[
             pltpu.VMEM((NP, PART, R), bf16),

time: 94.2 us -> 73.8 us (0.78)
  Pallas kernels: 81.5 us -> 68.7 us
  local copies, waits for them, and re-layouts: 11.9 us -> 3.4 us
    pallas_call x1, Pallas kernels: 81.5 us -> 68.7 us  [body(): pl.pallas_call(kernel, out_shape=pltpu.VMEM((N_COL, N_ROW, R, R), jnp.flo...]
    unnamed x7 -> x1, local copies, waits for them, and re-layouts: 11.9 us -> 3.4 us
where the time goes in v2:
time: 73.8 us; the launch traced here: 72.7 us
  Pallas kernels  68.7 us (93%)
  local copies, waits for them, and re-layouts  3.4 us (5%)
    pallas_call x1, Pallas kernels, body(): pl.pallas_call(kernel, out_shape=pltpu.VMEM((N_COL, N_ROW, R, R), jnp.flo...  68.7 us
    unnamed x1, local copies, waits for them, and re-layouts  3.4 us

profile of v2, /device:TPU:1, one launch (start us, length us, event | category | flops | bytes accessed | tf_op | source)
XLA Modules:
  0.0 72.7 jit_solution(15407762422856689268)
XLA Ops:
  0.7 68.7 %shard_map.55 = f32[16,8,128,128]{3,2,1,0:T(8,128)S(1)} custom-call(s32[128]{0:T(128)} %owner_ref.1, s32[1]{0:T(128)S(6)} %copy.8.rank_ref, bf16[16,96,128]{2,1,0:T(8,128)(2,1)} %panel_hbm.1, bf16[1536,1536]{1,0:T(8,128)(2,1)} %inverse_hbm.1, f32[16,8,128,128]{3,2,1,0:T(8,128)} %bitcast.3), custom_call_target="tpu_custom_call" | custom-call | flops 6442450944 | bytes 16777216 | tf_op jit(solution)/shard_map/pallas_call | solution.py:290
  69.3 3.4 %copy.7 = f32[1,1,16,8,128,128]{5,4,3,2,1,0:T(8,128)} copy(f32[1,1,16,8,128,128]{5,4,3,2,1,0:T(8,128)S(1)} %bitcast.2) | data formatting | bytes 16777216

commit v3 on v2

--- a/solution.py
+++ b/solution.py
@@ -13,14 +13,13 @@
 ROWS = B // N_COL
 PART = 16
 PARTS = ROWS // PART
-HB = B // 2
-HR = R // 2
+CUTS = 4
 MESH = pl.DeviceIdType.MESH
 
 
 def kernel(owner_ref, rank_ref, panel_hbm, inverse_hbm, cores_hbm, out_ref,
-           spread, moved, held_rows, held, inverse, rank_mine, rank_rows, rank_pack, rank_all,
-           right, left, send_sem, local_sem, sem_spread, sem_rank_a, sem_rank_b, sem_back, sem_rows,
+           spread, moved, held, inverse, rank_mine, rank_rows, rank_pack, rank_all,
+           right, left, send_sem, local_sem, sem_spread, sem_rank_a, sem_rank_b, sem_moved, sem_rows,
            sem_right, sem_left):
     r = lax.axis_index("row")
     c = lax.axis_index("col")
@@ -87,44 +86,41 @@
             moved[p] = spread[owner_ref[p]]
 
     for d in range(1, N_ROW):
-        to = (r + d) % N_ROW
-        send(moved.at[pl.ds(to * N_COL, N_COL)], held_rows.at[:, own_part, :],
-             sem_back.at[my_part], to, c, active)
-    own_back = pltpu.make_async_copy(
-        moved.at[pl.ds(r * N_COL, N_COL)], held_rows.at[:, own_part, :], local_sem.at[2])
-    pl.when(active)(own_back.start)
-
-    for d in range(1, N_ROW):
         frm = (r + d) % N_ROW
         arrived(rank_rows.at[frm], sem_rank_a.at[frm])
+    me = r * N_COL + c
+    own_rows = pl.ds(pl.multiple_of(c * ROWS + jnp.minimum(my_part, PARTS - 1) * PART, PART), PART)
+    own_copy = pltpu.make_async_copy(moved.at[me], held.at[own_rows, :], local_sem.at[2])
+
+    @pl.when(active)
+    def _():
+        @pl.loop(1, NP)
+        def _(d):
+            p = (me + d) % NP
+            pltpu.make_async_remote_copy(
+                src_ref=moved.at[p], dst_ref=held.at[own_rows, :],
+                send_sem=sem_moved.at[0], recv_sem=sem_rows.at[0],
+                device_id={"row": p // N_COL, "col": p % N_COL}, device_id_type=MESH).start()
+        own_copy.start()
+
     for k in range(N_ROW):
         rank_pack[pl.ds(k, 1), :] = rank_rows[k, pl.ds(0, 1), :]
     for d in range(1, N_COL):
         send(rank_pack, rank_all.at[c], sem_rank_b.at[c], r, (c + d) % N_COL)
     rank_all[c] = rank_pack[...]
-
-    pl.when(active)(own_back.wait)
-    for part in range(PARTS):
-        frm = (part + c + 1) % N_ROW
-
-        @pl.when(frm != r)
-        def _(part=part):
-            arrived(held_rows.at[:, pl.ds(part * PART, PART), :], sem_back.at[part])
-
-    for d in range(1, N_COL):
-        to = (c + d) % N_COL
-        send(held_rows.at[to], held.at[pl.ds(pl.multiple_of(c * ROWS, 16), ROWS), :], sem_rows.at[c], r, to)
-    own_rows = pltpu.make_async_copy(
-        held_rows.at[c], held.at[pl.ds(pl.multiple_of(c * ROWS, 16), ROWS), :], local_sem.at[2])
-    own_rows.start()
     for d in range(1, N_COL):
         frm = (c + d) % N_COL
         arrived(rank_all.at[frm], sem_rank_b.at[frm])
     inverse_copy.wait()
-    own_rows.wait()
-    for d in range(1, N_COL):
-        frm = (c + d) % N_COL
-        arrived(held.at[pl.ds(pl.multiple_of(frm * ROWS, 16), ROWS), :], sem_rows.at[frm])
+
+    @pl.when(active)
+    def _():
+        own_copy.wait()
+        arrived(held.at[pl.ds(0, B - PART), :], sem_rows.at[0])
+
+    @pl.when(jnp.logical_not(active))
+    def _():
+        arrived(held, sem_rows.at[0])
 
     block = owner_ref[r * N_COL + c]
     rank = rank_all[block % N_COL, pl.ds(block // N_COL, 1), :]
@@ -147,7 +143,7 @@
     sibling = col_of(0, 0, 1)
 
     def half(ref, slot, part):
-        size = HB if ref is right else HR
+        size = ref.shape[1] // CUTS
         return ref.at[slot, pl.ds(part * size, size), :]
 
     def send_right(slot, part, dx, flip=0):
@@ -186,92 +182,119 @@
     near_q = (row_of(-1, 1), row_of(1, 1))
     flip_far = (row_of(0, 1), row_of(2, 1))
     r_q, c_q = row_of(0, 1), col_of(0, 1)
-    toward = ((0, 1), (1, -1))
+    toward = ((0, 1), (2, -1))
+    order = (0, 2, 1, 3)
+
+    def near_right(flip, part, d, on):
+        wait_right(row_of(-d, flip), part)
+        if on:
+            send_right(row_of(-d, flip), part, d)
+
+    def near_left(flip, part, d, on):
+        wait_left(col_of(-d, flip), part)
+        if on:
+            send_left(col_of(-d, flip), part, d)
+
+    def near(flip, step):
+        for first, d in toward:
+            part = (first + step) % CUTS
+            near_right(flip, part, d, step < 2)
+            near_left(flip, part, d, step < 2)
+
+    def near_flip(part):
+        for first, d in toward:
+            on = part - first in (0, 1)
+            near_right(1, part, d, on)
+            near_left(1, part, d, on)
+
+    def flip_left(part):
+        wait_left(c_q, part)
+        for d in (1, -1):
+            send_left(c_q, part, d)
+
+    def flip_right(part):
+        wait_right(r_q, part)
+        for d in (1, -1):
+            send_right(r_q, part, d)
+
+    def far(flip, step):
+        for first, d in toward:
+            wait_right(row_of(2, flip), first + step)
+            wait_left(col_of(2, flip), first + step)
+
+    def grams(pairs, *rights):
+        for pair in pairs:
+            for pick in rights:
+                gram(pair, *pick)
 
     send_left(c, 0, 0, 1)
     send_right(r, 0, 0, 1)
-    for part, d in toward:
-        send_right(r, part, d)
-        send_left(c, part, d)
-    for part, d in toward:
-        send_right(r, 1 - part, d)
-        send_left(c, 1 - part, d)
-    send_left(c, 1, 0, 1)
-    send_right(r, 1, 0, 1)
+    for step in range(CUTS):
+        for first, d in toward:
+            send_right(r, (first + step) % CUTS, d)
+            send_left(c, (first + step) % CUTS, d)
+        if step:
+            send_left(c, order[step], 0, 1)
+            send_right(r, order[step], 0, 1)
     share(c)
-
-    for part, d in toward:
-        wait_right(row_of(-d, 0), part)
-        send_right(row_of(-d, 0), part, d)
-        wait_left(col_of(-d, 0), part)
-        send_left(col_of(-d, 0), part, d)
-    wait_left(c_q, 0)
-    for d in (1, -1):
-        send_left(c_q, 0, d)
-    wait_right(r_q, 0)
-    for d in (1, -1):
-        send_right(r_q, 0, d)
+    here, here_q, away, away_q = pair_of(0, 0), pair_of(0, 1), pair_of(2, 0), pair_of(2, 1)
+    beside = (pair_of(-1, 0), pair_of(1, 0))
+    beside_q = (pair_of(-1, 1), pair_of(1, 1))
+
+    near(0, 0)
+    flip_left(0)
+    near(0, 1)
+    flip_right(0)
     cores_copy.wait()
     wait_shared(col_of(0, 0, 1))
-
-    for part, d in toward:
-        wait_right(row_of(-d, 0), 1 - part)
-        wait_left(col_of(-d, 0), 1 - part)
-        share(col_of(-d, 0))
-    gram(pair_of(0, 0), *near_o)
-
-    wait_left(c_q, 1)
+    near(0, 2)
+    flip_left(2)
+    near(0, 3)
+    flip_right(2)
     for d in (1, -1):
-        send_left(c_q, 1, d)
+        share(col_of(d, 0))
+    far(0, 0)
+    flip_left(1)
+    grams((here,), near_o)
+    near_flip(0)
+    flip_right(1)
+    for d in (1, -1):
+        wait_shared(col_of(d, 0, 1))
+    grams(beside, near_o)
+    far(0, 1)
+    share(col_of(2, 0))
+    flip_left(3)
     share(c_q)
-    for part in range(2):
-        wait_right(row_of(2, 0), part)
-        wait_left(col_of(2, 0), part)
-    share(col_of(2, 0))
-    for d in (-1, 1):
-        wait_shared(col_of(d, 0, 1))
-        gram(pair_of(d, 0), *near_o)
-    wait_right(r_q, 1)
+    grams((here,), own_far)
+    near_flip(2)
+    flip_right(3)
+    grams(beside, own_far)
+    near_flip(1)
+    wait_shared(col_of(2, 0, 1))
+    grams((away,), near_o, own_far)
+    wait_shared(col_of(0, 1, 1))
+    near_flip(3)
     for d in (1, -1):
-        send_right(r_q, 1, d)
-
-    wait_shared(col_of(0, 1, 1))
-    gram(pair_of(0, 1), *near_o)
-    gram(pair_of(0, 1), *own_far)
-    gram(pair_of(0, 0), *own_far)
-    for part, d in toward:
-        wait_left(col_of(-d, 1), part)
-        send_left(col_of(-d, 1), part, d)
-    wait_shared(col_of(2, 0, 1))
-    gram(pair_of(2, 0), *near_o)
-    gram(pair_of(2, 0), *own_far)
-    for part, d in toward:
-        wait_right(row_of(-d, 1), part)
-        send_right(row_of(-d, 1), part, d)
-    for d in (-1, 1):
-        gram(pair_of(d, 0), *own_far)
-    for part, d in toward:
-        wait_left(col_of(-d, 1), 1 - part)
-        share(col_of(-d, 1))
-    for d in (-1, 1):
+        share(col_of(d, 1))
+    grams((here_q,), near_o, own_far)
+    grams((here, here_q), near_q)
+    far(1, 0)
+    grams(beside + (away,), near_q)
+    for d in (1, -1):
         wait_shared(col_of(d, 1, 1))
-        gram(pair_of(d, 1), *near_o)
-        gram(pair_of(d, 1), *own_far)
-    for part, d in toward:
-        wait_right(row_of(-d, 1), 1 - part)
-    for pair in (pair_of(0, 0), pair_of(0, 1), pair_of(2, 0), pair_of(-1, 0), pair_of(1, 0), pair_of(-1, 1), pair_of(1, 1)):
-        gram(pair, *near_q)
-
-    for part in range(2):
-        wait_left(col_of(2, 1), part)
+    far(1, 1)
     share(col_of(2, 1))
-    for part in range(2):
-        wait_right(row_of(2, 1), part)
-    for pair in (pair_of(0, 0), pair_of(0, 1), pair_of(2, 0), pair_of(-1, 0), pair_of(1, 0), pair_of(-1, 1), pair_of(1, 1)):
-        gram(pair, *flip_far)
+    grams(beside_q, near_o, own_far, near_q)
+    grams((here, here_q, away) + beside + beside_q, flip_far)
     wait_shared(col_of(2, 1, 1))
-    for rights in (near_o, own_far, near_q, flip_far):
-        gram(pair_of(2, 1), *rights)
+    grams((away_q,), near_o, own_far, near_q, flip_far)
+
+    @pl.when(active)
+    def _():
+        pltpu.make_async_remote_copy(
+            src_ref=moved.at[pl.ds(0, NP - 1)], dst_ref=moved.at[pl.ds(0, NP - 1)],
+            send_sem=sem_moved.at[0], recv_sem=sem_moved.at[0],
+            device_id={"row": r, "col": c}, device_id_type=MESH).wait_send()
 
     for desc, when in sends:
         if when is None:
@@ -295,7 +318,6 @@
         scratch_shapes=[
             pltpu.VMEM((NP, PART, R), bf16),
             pltpu.VMEM((NP, PART, R), bf16),
-            pltpu.VMEM((N_COL, ROWS, R), bf16),
             pltpu.VMEM((B, R), bf16),
             pltpu.VMEM((B, B), bf16),
             pltpu.VMEM((8, R), jnp.int32),
@@ -304,15 +326,15 @@
             pltpu.VMEM((N_COL, 8, R), jnp.int32),
             pltpu.VMEM((N_ROW, B, R), bf16),
             pltpu.VMEM((N_COL, R, B), bf16),
-            dma((96,)),
+            dma((128,)),
             dma((3,)),
             dma((N_ROW,)),
             dma((N_ROW,)),
             dma((N_COL,)),
-            dma((N_ROW,)),
-            dma((N_COL,)),
-            dma((N_ROW, 2)),
-            dma((N_COL, 2)),
+            dma((1,)),
+            dma((1,)),
+            dma((N_ROW, CUTS)),
+            dma((N_COL, CUTS)),
         ],
         compiler_params=pltpu.CompilerParams(
             collective_id=0, has_side_effects=True, vmem_limit_bytes=48 << 20),

time: 73.8 us -> 68.4 us (0.927); the launches traced: 72.7 us -> 68.2 us
  Pallas kernels: 68.7 us -> 64.2 us
    pallas_call x1, Pallas kernels: 68.7 us -> 64.2 us  [body(): pl.pallas_call(kernel, out_shape=pltpu.VMEM((N_COL, N_ROW, R, R), jnp.flo...]
where the time goes in v3:
time: 68.4 us; the launch traced here: 68.2 us
  Pallas kernels  64.2 us (94%)
  local copies, waits for them, and re-layouts  3.4 us (5%)
    pallas_call x1, Pallas kernels, body(): pl.pallas_call(kernel, out_shape=pltpu.VMEM((N_COL, N_ROW, R, R), jnp.flo...  64.2 us
    unnamed x1, local copies, waits for them, and re-layouts  3.4 us

profile of v3, /device:TPU:1, one launch (start us, length us, event | category | flops | bytes accessed | tf_op | source)
XLA Modules:
  0.0 68.2 jit_solution(17660479641478511)
XLA Ops:
  0.7 64.2 %shard_map.55 = f32[16,8,128,128]{3,2,1,0:T(8,128)S(1)} custom-call(s32[128]{0:T(128)} %owner_ref.1, s32[1]{0:T(128)S(6)} %copy.8.rank_ref, bf16[16,96,128]{2,1,0:T(8,128)(2,1)} %panel_hbm.1, bf16[1536,1536]{1,0:T(8,128)(2,1)} %inverse_hbm.1, f32[16,8,128,128]{3,2,1,0:T(8,128)} %bitcast.3), custom_call_target="tpu_custom_call" | custom-call | flops 6442450944 | bytes 16777216 | tf_op jit(solution)/shard_map/pallas_call | solution.py:313
  64.8 3.4 %copy.7 = f32[1,1,16,8,128,128]{5,4,3,2,1,0:T(8,128)} copy(f32[1,1,16,8,128,128]{5,4,3,2,1,0:T(8,128)S(1)} %bitcast.2) | data formatting | bytes 16777216

commit v4 on v3

--- a/solution.py
+++ b/solution.py
@@ -15,11 +15,82 @@
 PARTS = ROWS // PART
 CUTS = 4
 MESH = pl.DeviceIdType.MESH
-
-
-def kernel(owner_ref, rank_ref, panel_hbm, inverse_hbm, cores_hbm, out_ref,
+NEAR, FAR, FLIP, RELAY, SHARE, WAIT, GRAM = range(7)
+RIGHT, LEFT = 0, 1
+Z_ORDER = (
+    (LEFT, 0), (RIGHT, 0), (LEFT, 2), (RIGHT, 2), (LEFT, 1), (RIGHT, 1), (LEFT, 3), (RIGHT, 3),
+)
+STEPS = (
+    (NEAR, RIGHT, 0, 1, 1), (FLIP, LEFT, 0), (FLIP, LEFT, 2), (NEAR, RIGHT, 0, -1, 2),
+    (NEAR, LEFT, 0, -1, 3), (NEAR, LEFT, 0, 1, 0), (NEAR, LEFT, 0, -1, 2), (FLIP, RIGHT, 2),
+    (FLIP, RIGHT, 0), (NEAR, LEFT, 0, 1, 1), (FLIP, LEFT, 1), (NEAR, LEFT, 0, -1, 0),
+    (NEAR, RIGHT, 0, 1, 3), (NEAR, LEFT, 1, -1, 0), (FLIP, RIGHT, 1), (NEAR, LEFT, 0, 1, 2),
+    (NEAR, RIGHT, 1, 1, 2), (NEAR, LEFT, 0, -1, 1), (FLIP, LEFT, 3), (NEAR, LEFT, 0, 1, 3),
+    (NEAR, RIGHT, 0, -1, 1), (NEAR, RIGHT, 0, 1, 0), (NEAR, RIGHT, 0, -1, 3), (NEAR, LEFT, 1, 1, 0),
+    (SHARE, 3, 0), (SHARE, 1, 0), (RELAY, 3), (SHARE, 0, 1),
+    (FLIP, RIGHT, 3), (FAR, LEFT, 0), (RELAY, 1), (NEAR, LEFT, 1, -1, 2),
+    (NEAR, RIGHT, 1, -1, 2), (SHARE, 2, 0), (WAIT, 0, 0), (NEAR, RIGHT, 0, 1, 2),
+    (WAIT, 0, 1), (NEAR, RIGHT, 1, -1, 1), (NEAR, LEFT, 1, 1, 2), (FAR, RIGHT, 0),
+    (NEAR, RIGHT, 0, -1, 0), (NEAR, RIGHT, 1, 1, 0), (WAIT, 1, 0), (NEAR, LEFT, 1, -1, 1),
+    (NEAR, RIGHT, 1, -1, 0), (GRAM, 0, 1, 0), (NEAR, LEFT, 1, 1, 1), (WAIT, 3, 0),
+    (GRAM, 1, 0, 0), (GRAM, 3, 0, 1), (WAIT, 2, 0), (GRAM, 0, 0, 0),
+    (GRAM, 0, 0, 1), (NEAR, LEFT, 1, 1, 3), (GRAM, 2, 0, 0), (NEAR, LEFT, 1, -1, 3),
+    (SHARE, 1, 1), (SHARE, 3, 1), (NEAR, RIGHT, 1, -1, 3), (NEAR, RIGHT, 1, 1, 3),
+    (NEAR, RIGHT, 1, 1, 1), (GRAM, 1, 0, 1), (GRAM, 0, 1, 2), (GRAM, 0, 1, 1),
+    (GRAM, 0, 0, 2), (GRAM, 2, 0, 2), (FAR, LEFT, 1), (SHARE, 2, 1),
+    (GRAM, 3, 0, 0), (GRAM, 1, 0, 2), (GRAM, 2, 0, 1), (GRAM, 3, 0, 2),
+    (WAIT, 3, 1), (WAIT, 1, 1), (GRAM, 1, 1, 1), (GRAM, 1, 1, 0),
+    (GRAM, 3, 1, 1), (GRAM, 3, 1, 0), (FAR, RIGHT, 1), (WAIT, 2, 1),
+)
+
+
+def pair_at(y, zl, dy, flip):
+    return ((y + dy) % 4) * 2 + (1 - zl if flip else zl)
+
+
+def rights_at(x, zh):
+    def row_of(dx, flip):
+        return ((x + dx) % 4) * 2 + (1 - zh if flip else zh)
+
+    return (
+        (row_of(-1, 0), row_of(1, 0)),
+        (row_of(0, 0), row_of(2, 0)),
+        (row_of(-1, 1), row_of(1, 1)),
+        (row_of(0, 1), row_of(2, 1)),
+    )
+
+
+def gram(left, right, out, pair, first, second):
+    lhs = left[pl.ds(pair * 2, 2)].reshape(2 * R, B)
+    rhs = jnp.concatenate([right[first], right[second]], axis=1)
+    g = jnp.dot(lhs, rhs, preferred_element_type=jnp.float32)
+    for i in range(2):
+        for j, slot in enumerate((first, second)):
+            out[pair * 2 + i, slot] -= g[i * R:(i + 1) * R, j * R:(j + 1) * R]
+
+
+def finish(left, right, grams_in, out_hbm, grams, sem):
+    r = lax.axis_index("row")
+    c = lax.axis_index("col")
+    x, zh, y, zl = r // 2, r % 2, c // 4, (c // 2) % 2
+    done = {step[1:] for step in STEPS if step[0] == GRAM}
+    copies = []
+    for dy, flip in ((0, 0), (0, 1), (1, 0), (3, 0), (2, 0), (1, 1), (3, 1), (2, 1)):
+        pair = pair_at(y, zl, dy, flip)
+        for pick, rights in enumerate(rights_at(x, zh)):
+            if (dy, flip, pick) not in done:
+                gram(left, right, grams, pair, *rights)
+        rows = pl.ds(pair * 2, 2)
+        copy = pltpu.make_async_copy(grams.at[rows], out_hbm.at[rows], sem.at[len(copies)])
+        copy.start()
+        copies.append(copy)
+    for copy in copies:
+        copy.wait()
+
+
+def kernel(owner_ref, rank_ref, panel_hbm, inverse_hbm, cores_hbm, out_ref, right, left,
            spread, moved, held, inverse, rank_mine, rank_rows, rank_pack, rank_all,
-           right, left, send_sem, local_sem, sem_spread, sem_rank_a, sem_rank_b, sem_moved, sem_rows,
+           send_sem, local_sem, sem_spread, sem_rank_a, sem_rank_b, sem_moved, sem_rows,
            sem_right, sem_left):
     r = lax.axis_index("row")
     c = lax.axis_index("col")
@@ -27,9 +98,7 @@
     y, zl, h = c // 4, (c // 2) % 2, c % 2
 
     inverse_copy = pltpu.make_async_copy(inverse_hbm, inverse, local_sem.at[0])
-    inverse_copy.start()
     cores_copy = pltpu.make_async_copy(cores_hbm, out_ref, local_sem.at[1])
-    cores_copy.start()
 
     barrier = pltpu.get_barrier_semaphore()
     for d in range(1, N_ROW):
@@ -68,6 +137,7 @@
     own_spread = pltpu.make_async_copy(
         panel_hbm.at[:, own_part, :], spread.at[pl.ds(r * N_COL, N_COL)], local_sem.at[2])
     pl.when(active)(own_spread.start)
+    inverse_copy.start()
 
     rank_mine[...] = jnp.full((8, R), rank_ref[0], jnp.int32)
     for d in range(1, N_ROW):
@@ -80,10 +150,6 @@
         for d in range(1, N_ROW):
             frm = (r + d) % N_ROW
             arrived(spread.at[pl.ds(frm * N_COL, N_COL)], sem_spread.at[frm])
-
-        @pl.loop(0, NP, unroll=8)
-        def _(p):
-            moved[p] = spread[owner_ref[p]]
 
     for d in range(1, N_ROW):
         frm = (r + d) % N_ROW
@@ -97,11 +163,15 @@
         @pl.loop(1, NP)
         def _(d):
             p = (me + d) % NP
+            moved[p] = spread[owner_ref[p]]
             pltpu.make_async_remote_copy(
                 src_ref=moved.at[p], dst_ref=held.at[own_rows, :],
                 send_sem=sem_moved.at[0], recv_sem=sem_rows.at[0],
                 device_id={"row": p // N_COL, "col": p % N_COL}, device_id_type=MESH).start()
+        moved[me] = spread[owner_ref[me]]
         own_copy.start()
+
+    cores_copy.start()
 
     for k in range(N_ROW):
         rank_pack[pl.ds(k, 1), :] = rank_rows[k, pl.ds(0, 1), :]
@@ -166,128 +236,67 @@
     def wait_shared(slot):
         arrived(left.at[slot], sem_left.at[slot, 0])
 
-    def gram(pair, first, second):
-        lhs = left[pl.ds(pair * 2, 2)].reshape(2 * R, B)
-        rhs = jnp.concatenate([right[first], right[second]], axis=1)
-        g = jnp.dot(lhs, rhs, preferred_element_type=jnp.float32)
-        for i in range(2):
-            for j, slot in enumerate((first, second)):
-                out_ref[pair * 2 + i, slot] -= g[i * R:(i + 1) * R, j * R:(j + 1) * R]
-
-    def pair_of(dy, flip):
-        return ((y + dy) % 4) * 2 + (1 - zl if flip else zl)
-
-    near_o = (row_of(-1, 0), row_of(1, 0))
-    own_far = (row_of(0, 0), row_of(2, 0))
-    near_q = (row_of(-1, 1), row_of(1, 1))
-    flip_far = (row_of(0, 1), row_of(2, 1))
     r_q, c_q = row_of(0, 1), col_of(0, 1)
-    toward = ((0, 1), (2, -1))
-    order = (0, 2, 1, 3)
-
-    def near_right(flip, part, d, on):
-        wait_right(row_of(-d, flip), part)
-        if on:
-            send_right(row_of(-d, flip), part, d)
-
-    def near_left(flip, part, d, on):
-        wait_left(col_of(-d, flip), part)
-        if on:
-            send_left(col_of(-d, flip), part, d)
-
-    def near(flip, step):
-        for first, d in toward:
-            part = (first + step) % CUTS
-            near_right(flip, part, d, step < 2)
-            near_left(flip, part, d, step < 2)
-
-    def near_flip(part):
-        for first, d in toward:
-            on = part - first in (0, 1)
-            near_right(1, part, d, on)
-            near_left(1, part, d, on)
-
-    def flip_left(part):
-        wait_left(c_q, part)
-        for d in (1, -1):
-            send_left(c_q, part, d)
-
-    def flip_right(part):
-        wait_right(r_q, part)
-        for d in (1, -1):
-            send_right(r_q, part, d)
-
-    def far(flip, step):
-        for first, d in toward:
-            wait_right(row_of(2, flip), first + step)
-            wait_left(col_of(2, flip), first + step)
-
-    def grams(pairs, *rights):
-        for pair in pairs:
-            for pick in rights:
-                gram(pair, *pick)
-
-    send_left(c, 0, 0, 1)
-    send_right(r, 0, 0, 1)
+    z_order = list(Z_ORDER)
+
+    def along_z(count):
+        for kind, part in z_order[:count]:
+            if kind == RIGHT:
+                send_right(r, part, 0, 1)
+            else:
+                send_left(c, part, 0, 1)
+        del z_order[:count]
+
+    along_z(2)
     for step in range(CUTS):
-        for first, d in toward:
+        for first, d in ((0, 1), (2, -1)):
             send_right(r, (first + step) % CUTS, d)
             send_left(c, (first + step) % CUTS, d)
         if step:
-            send_left(c, order[step], 0, 1)
-            send_right(r, order[step], 0, 1)
+            along_z(2)
     share(c)
-    here, here_q, away, away_q = pair_of(0, 0), pair_of(0, 1), pair_of(2, 0), pair_of(2, 1)
-    beside = (pair_of(-1, 0), pair_of(1, 0))
-    beside_q = (pair_of(-1, 1), pair_of(1, 1))
-
-    near(0, 0)
-    flip_left(0)
-    near(0, 1)
-    flip_right(0)
     cores_copy.wait()
-    wait_shared(col_of(0, 0, 1))
-    near(0, 2)
-    flip_left(2)
-    near(0, 3)
-    flip_right(2)
-    for d in (1, -1):
-        share(col_of(d, 0))
-    far(0, 0)
-    flip_left(1)
-    grams((here,), near_o)
-    near_flip(0)
-    flip_right(1)
-    for d in (1, -1):
-        wait_shared(col_of(d, 0, 1))
-    grams(beside, near_o)
-    far(0, 1)
-    share(col_of(2, 0))
-    flip_left(3)
-    share(c_q)
-    grams((here,), own_far)
-    near_flip(2)
-    flip_right(3)
-    grams(beside, own_far)
-    near_flip(1)
-    wait_shared(col_of(2, 0, 1))
-    grams((away,), near_o, own_far)
-    wait_shared(col_of(0, 1, 1))
-    near_flip(3)
-    for d in (1, -1):
-        share(col_of(d, 1))
-    grams((here_q,), near_o, own_far)
-    grams((here, here_q), near_q)
-    far(1, 0)
-    grams(beside + (away,), near_q)
-    for d in (1, -1):
-        wait_shared(col_of(d, 1, 1))
-    far(1, 1)
-    share(col_of(2, 1))
-    grams(beside_q, near_o, own_far, near_q)
-    grams((here, here_q, away) + beside + beside_q, flip_far)
-    wait_shared(col_of(2, 1, 1))
-    grams((away_q,), near_o, own_far, near_q, flip_far)
+
+    for step, *rest in STEPS:
+        if step == NEAR:
+            kind, flip, d, part = rest
+            on = part // 2 == (0 if d == 1 else 1)
+            if kind == RIGHT:
+                wait_right(row_of(-d, flip), part)
+                if on:
+                    send_right(row_of(-d, flip), part, d)
+            else:
+                wait_left(col_of(-d, flip), part)
+                if on and not (flip and part % 2):
+                    send_left(col_of(-d, flip), part, d)
+        elif step == FLIP:
+            kind, part = rest
+            if kind == RIGHT:
+                wait_right(r_q, part)
+            else:
+                wait_left(c_q, part)
+            for d in (1, -1):
+                if kind == RIGHT:
+                    send_right(r_q, part, d)
+                else:
+                    send_left(c_q, part, d)
+        elif step == RELAY:
+            wait_left(col_of(2, 0), rest[0])
+            send_left(col_of(2, 0), rest[0], 0, 1)
+        elif step == FAR:
+            kind, flip = rest
+            for part in range(CUTS):
+                if kind == RIGHT:
+                    wait_right(row_of(2, flip), part)
+                elif flip or part % 2 == 0:
+                    wait_left(col_of(2, flip), part)
+        elif step == SHARE:
+            share(col_of(*rest))
+        elif step == WAIT:
+            wait_shared(col_of(*rest, 1))
+        else:
+            dy, flip, pick = rest
+            gram(left, right, out_ref, pair_at(y, zl, dy, flip), *rights_at(x, zh)[pick])
 
     @pl.when(active)
     def _():
@@ -310,11 +319,15 @@
     hbm = pl.BlockSpec(memory_space=pltpu.HBM)
     bf16 = jnp.bfloat16
     dma = pltpu.SemaphoreType.DMA
-    out = pl.pallas_call(
+    out, right, left = pl.pallas_call(
         kernel,
-        out_shape=pltpu.VMEM((N_COL, N_ROW, R, R), jnp.float32),
+        out_shape=(
+            pltpu.VMEM((N_COL, N_ROW, R, R), jnp.float32),
+            pltpu.VMEM((N_ROW, B, R), bf16),
+            pltpu.VMEM((N_COL, R, B), bf16),
+        ),
         in_specs=[smem, smem, hbm, hbm, hbm],
-        out_specs=vmem,
+        out_specs=(vmem, vmem, vmem),
         scratch_shapes=[
             pltpu.VMEM((NP, PART, R), bf16),
             pltpu.VMEM((NP, PART, R), bf16),
@@ -324,8 +337,6 @@
             pltpu.VMEM((N_ROW, 8, R), jnp.int32),
             pltpu.VMEM((8, R), jnp.int32),
             pltpu.VMEM((N_COL, 8, R), jnp.int32),
-            pltpu.VMEM((N_ROW, B, R), bf16),
-            pltpu.VMEM((N_COL, R, B), bf16),
             dma((128,)),
             dma((3,)),
             dma((N_ROW,)),
@@ -337,10 +348,20 @@
             dma((N_COL, CUTS)),
         ],
         compiler_params=pltpu.CompilerParams(
-            collective_id=0, has_side_effects=True, vmem_limit_bytes=48 << 20),
+            collective_id=0, has_side_effects=True, vmem_limit_bytes=(46 << 20) + (512 << 10)),
         cost_estimate=pl.CostEstimate(
             flops=2 * grams * B, bytes_accessed=4 * grams * 2, transcendentals=0),
     )(owner_map, ranks, panel_right, factor_inverse, cores.reshape(N_COL, N_ROW, R, R))
+    here = [pltpu.with_memory_space_constraint(v, pltpu.VMEM) for v in (left, right, out)]
+    out, _ = pl.pallas_call(
+        finish,
+        out_shape=(jax.ShapeDtypeStruct(out.shape, jnp.float32), pltpu.VMEM(out.shape, jnp.float32)),
+        in_specs=[vmem, vmem, vmem],
+        out_specs=(hbm, vmem),
+        input_output_aliases={2: 1},
+        scratch_shapes=[dma((N_COL // 2,))],
+        compiler_params=pltpu.CompilerParams(vmem_limit_bytes=8 << 20),
+    )(*here)
     return out.reshape(cores.shape)
 
 

time: 68.4 us -> 64.8 us (0.947)
  local copies, waits for them, and re-layouts: 3.4 us -> 0 us
    unnamed x1 -> x0, local copies, waits for them, and re-layouts: 3.4 us -> none
    pallas_call x1 -> x2, Pallas kernels: 64.2 us -> 63.6 us  [the longest x1 59.7 us: body(): pl.pallas_call(kernel, out_shape=(pltpu.VMEM((N_COL, N_ROW, R, R), jnp.fl...]
where the time goes in v4:
time: 64.8 us; the launch traced here: 64.3 us
  Pallas kernels  63.6 us (98%)
  between operations  0.66 us (1%)
    pallas_call x1, Pallas kernels, body(): pl.pallas_call(kernel, out_shape=(pltpu.VMEM((N_COL, N_ROW, R, R), jnp.fl...  59.7 us
    pallas_call x1, Pallas kernels, body(): pl.pallas_call(finish, out_shape=(jax.ShapeDtypeStruct(out.shape, jnp.flo...  3.91 us

profile of v4, /device:TPU:1, one launch (start us, length us, event | category | flops | bytes accessed | tf_op | source)
XLA Modules:
  0.0 64.3 jit_solution(2082176067916823858)
XLA Ops:
  0.7 59.7 %shard_map.55 = (f32[16,8,128,128]{3,2,1,0:T(8,128)S(1)}, bf16[8,1536,128]{2,1,0:T(8,128)(2,1)S(1)}, bf16[16,128,1536]{2,1,0:T(8,128)(2,1)S(1)}) custom-call(s32[128]{0:T(128)} %owner_ref.1, s32[1]{0:T(128)S(6)} %copy.8.rank_ref, bf16[16,96,128]{2,1,0:T(8,128)(2,1)} %panel_hbm.1, bf16[1536,1536]{1,0:T(8,128)(2,1)} %inverse_hbm.1, f32[16,8,128,128]{3,2,1,0:T(8,128)} %bitcast.2), custom_call_target="tpu_custom_call" | custom-call | flops 6442450944 | bytes 16777216 | tf_op jit(solution)/shard_map/pallas_call | solution.py:322
  60.3 3.9 %shard_map.56 = (f32[16,8,128,128]{3,2,1,0:T(8,128)}, f32[16,8,128,128]{3,2,1,0:T(8,128)S(1)}) custom-call(bf16[16,128,1536]{2,1,0:T(8,128)(2,1)S(1)} %get-tuple-element.9.left, bf16[8,1536,128]{2,1,0:T(8,128)(2,1)S(1)} %get-tuple-element.10.right, f32[16,8,128,128]{3,2,1,0:T(8,128)S(1)} %get-tuple-element.11.grams_in), custom_call_target="tpu_custom_call", output_to_operand_aliasing={{1}: (2, {})} | custom-call | tf_op jit(solution)/shard_map/pallas_call | solution.py:356

commit v5 on v4

--- a/solution.py
+++ b/solution.py
@@ -88,8 +88,8 @@
         copy.wait()
 
 
-def kernel(owner_ref, rank_ref, panel_hbm, inverse_hbm, cores_hbm, out_ref, right, left,
-           spread, moved, held, inverse, rank_mine, rank_rows, rank_pack, rank_all,
+def kernel(owner_hbm, rank_hbm, panel_hbm, inverse_hbm, cores_hbm, out_ref, right, left,
+           owner_ref, rank_ref, panel, spread, moved, held, inverse, rank_mine, rank_rows, rank_pack, rank_all,
            send_sem, local_sem, sem_spread, sem_rank_a, sem_rank_b, sem_moved, sem_rows,
            sem_right, sem_left):
     r = lax.axis_index("row")
@@ -97,29 +97,38 @@
     x, zh = r // 2, r % 2
     y, zl, h = c // 4, (c // 2) % 2, c % 2
 
-    inverse_copy = pltpu.make_async_copy(inverse_hbm, inverse, local_sem.at[0])
-    cores_copy = pltpu.make_async_copy(cores_hbm, out_ref, local_sem.at[1])
-
     barrier = pltpu.get_barrier_semaphore()
     for d in range(1, N_ROW):
         pl.semaphore_signal(barrier, inc=1, device_id={"row": (r + d) % N_ROW, "col": c}, device_id_type=MESH)
     for d in range(1, N_COL):
         pl.semaphore_signal(barrier, inc=1, device_id={"row": r, "col": (c + d) % N_COL}, device_id_type=MESH)
+    inverse_copy = pltpu.make_async_copy(inverse_hbm, inverse, local_sem.at[0])
+    cores_copy = pltpu.make_async_copy(cores_hbm, out_ref, local_sem.at[1])
+    panel_copy = pltpu.make_async_copy(panel_hbm, panel, local_sem.at[3])
+    rank_copy = pltpu.make_async_copy(rank_hbm, rank_ref, local_sem.at[4])
+    owner_copy = pltpu.make_async_copy(owner_hbm, owner_ref, local_sem.at[5])
+    for copy in (panel_copy, rank_copy, owner_copy):
+        copy.start()
+    panel_copy.wait()
     pl.semaphore_wait(barrier, N_ROW + N_COL - 2)
 
-    sends = []
-    counter = [0]
-
-    def send(src, dst, recv, row, col, when=None):
+    SPREAD, RANK_A, RANK_B, TO_ROW, TO_COL = range(5)
+    sent = [0] * 5
+
+    def send(src, dst, recv, row, col, group, when=None):
         desc = pltpu.make_async_remote_copy(
-            src_ref=src, dst_ref=dst, send_sem=send_sem.at[counter[0]], recv_sem=recv,
+            src_ref=src, dst_ref=dst, send_sem=send_sem.at[group], recv_sem=recv,
             device_id={"row": row, "col": col}, device_id_type=MESH)
-        counter[0] += 1
+        sent[group] += src.shape[-3] if len(src.shape) == 3 else src.shape[-2]
         if when is None:
             desc.start()
         else:
             pl.when(when)(desc.start)
-        sends.append((desc, when))
+
+    def left_device(ref, sem):
+        pltpu.make_async_remote_copy(
+            src_ref=ref, dst_ref=ref, send_sem=sem, recv_sem=sem,
+            device_id={"row": r, "col": c}, device_id_type=MESH).wait_send()
 
     def arrived(dst, recv):
         pltpu.make_async_remote_copy(
@@ -131,18 +140,20 @@
     for d in range(1, N_ROW):
         to = (r + d) % N_ROW
         part = (to - c - 1) % N_ROW
-        send(panel_hbm.at[:, pl.ds(pl.multiple_of(jnp.minimum(part, PARTS - 1) * PART, PART), PART), :],
-             spread.at[pl.ds(r * N_COL, N_COL)], sem_spread.at[r], to, c, part < PARTS)
+        send(panel.at[:, pl.ds(pl.multiple_of(jnp.minimum(part, PARTS - 1) * PART, PART), PART), :],
+             spread.at[pl.ds(r * N_COL, N_COL)], sem_spread.at[r], to, c, SPREAD, part < PARTS)
     own_part = pl.ds(pl.multiple_of(jnp.minimum(my_part, PARTS - 1) * PART, PART), PART)
     own_spread = pltpu.make_async_copy(
-        panel_hbm.at[:, own_part, :], spread.at[pl.ds(r * N_COL, N_COL)], local_sem.at[2])
+        panel.at[:, own_part, :], spread.at[pl.ds(r * N_COL, N_COL)], local_sem.at[2])
     pl.when(active)(own_spread.start)
     inverse_copy.start()
 
+    rank_copy.wait()
     rank_mine[...] = jnp.full((8, R), rank_ref[0], jnp.int32)
     for d in range(1, N_ROW):
-        send(rank_mine, rank_rows.at[r], sem_rank_a.at[r], (r + d) % N_ROW, c)
+        send(rank_mine, rank_rows.at[r], sem_rank_a.at[r], (r + d) % N_ROW, c, RANK_A)
     rank_rows[r] = rank_mine[...]
+    owner_copy.wait()
 
     @pl.when(active)
     def _():
@@ -151,9 +162,6 @@
             frm = (r + d) % N_ROW
             arrived(spread.at[pl.ds(frm * N_COL, N_COL)], sem_spread.at[frm])
 
-    for d in range(1, N_ROW):
-        frm = (r + d) % N_ROW
-        arrived(rank_rows.at[frm], sem_rank_a.at[frm])
     me = r * N_COL + c
     own_rows = pl.ds(pl.multiple_of(c * ROWS + jnp.minimum(my_part, PARTS - 1) * PART, PART), PART)
     own_copy = pltpu.make_async_copy(moved.at[me], held.at[own_rows, :], local_sem.at[2])
@@ -173,10 +181,13 @@
 
     cores_copy.start()
 
+    for d in range(1, N_ROW):
+        frm = (r + d) % N_ROW
+        arrived(rank_rows.at[frm], sem_rank_a.at[frm])
     for k in range(N_ROW):
         rank_pack[pl.ds(k, 1), :] = rank_rows[k, pl.ds(0, 1), :]
     for d in range(1, N_COL):
-        send(rank_pack, rank_all.at[c], sem_rank_b.at[c], r, (c + d) % N_COL)
+        send(rank_pack, rank_all.at[c], sem_rank_b.at[c], r, (c + d) % N_COL, RANK_B)
     rank_all[c] = rank_pack[...]
     for d in range(1, N_COL):
         frm = (c + d) % N_COL
@@ -218,14 +229,14 @@
 
     def send_right(slot, part, dx, flip=0):
         ref = half(right, slot, part)
-        send(ref, ref, sem_right.at[slot, part], row_of(dx, flip), c)
+        send(ref, ref, sem_right.at[slot, part], row_of(dx, flip), c, TO_ROW)
 
     def send_left(slot, part, dy, flip=0):
         ref = half(left, slot, part)
-        send(ref, ref, sem_left.at[slot, part], r, col_of(dy, flip))
+        send(ref, ref, sem_left.at[slot, part], r, col_of(dy, flip), TO_COL)
 
     def share(slot):
-        send(left.at[slot], left.at[slot], sem_left.at[slot, 0], r, sibling)
+        send(left.at[slot], left.at[slot], sem_left.at[slot, 0], r, sibling, TO_COL)
 
     def wait_right(slot, part):
         arrived(half(right, slot, part), sem_right.at[slot, part])
@@ -298,24 +309,26 @@
             dy, flip, pick = rest
             gram(left, right, out_ref, pair_at(y, zl, dy, flip), *rights_at(x, zh)[pick])
 
+    assert sent[TO_ROW] % B == 0 and sent[TO_COL] % R == 0
+
     @pl.when(active)
     def _():
-        pltpu.make_async_remote_copy(
-            src_ref=moved.at[pl.ds(0, NP - 1)], dst_ref=moved.at[pl.ds(0, NP - 1)],
-            send_sem=sem_moved.at[0], recv_sem=sem_moved.at[0],
-            device_id={"row": r, "col": c}, device_id_type=MESH).wait_send()
-
-    for desc, when in sends:
-        if when is None:
-            desc.wait_send()
-        else:
-            pl.when(when)(desc.wait_send)
+        left_device(moved.at[pl.ds(0, NP - 1)], sem_moved.at[0])
+        left_device(spread.at[pl.ds(0, (PARTS - 1) * N_COL)], send_sem.at[SPREAD])
+
+    @pl.when(jnp.logical_not(active))
+    def _():
+        left_device(spread.at[pl.ds(0, PARTS * N_COL)], send_sem.at[SPREAD])
+
+    left_device(rank_rows.at[pl.ds(0, N_ROW - 1)], send_sem.at[RANK_A])
+    left_device(rank_all.at[pl.ds(0, N_COL - 1)], send_sem.at[RANK_B])
+    left_device(right.at[pl.ds(0, sent[TO_ROW] // B)], send_sem.at[TO_ROW])
+    left_device(left.at[pl.ds(0, sent[TO_COL] // R)], send_sem.at[TO_COL])
 
 
 def body(panel_right, factor_inverse, ranks, owner_map, cores):
     grams = 16 * 8 * 128 * 128
     vmem = pl.BlockSpec(memory_space=pltpu.VMEM)
-    smem = pl.BlockSpec(memory_space=pltpu.SMEM)
     hbm = pl.BlockSpec(memory_space=pltpu.HBM)
     bf16 = jnp.bfloat16
     dma = pltpu.SemaphoreType.DMA
@@ -326,9 +339,12 @@
             pltpu.VMEM((N_ROW, B, R), bf16),
             pltpu.VMEM((N_COL, R, B), bf16),
         ),
-        in_specs=[smem, smem, hbm, hbm, hbm],
+        in_specs=[hbm, hbm, hbm, hbm, hbm],
         out_specs=(vmem, vmem, vmem),
         scratch_shapes=[
+            pltpu.SMEM((NP,), jnp.int32),
+            pltpu.SMEM((1,), jnp.int32),
+            pltpu.VMEM((N_COL, ROWS, R), bf16),
             pltpu.VMEM((NP, PART, R), bf16),
             pltpu.VMEM((NP, PART, R), bf16),
             pltpu.VMEM((B, R), bf16),
@@ -337,8 +353,8 @@
             pltpu.VMEM((N_ROW, 8, R), jnp.int32),
             pltpu.VMEM((8, R), jnp.int32),
             pltpu.VMEM((N_COL, 8, R), jnp.int32),
-            dma((128,)),
-            dma((3,)),
+            dma((5,)),
+            dma((6,)),
             dma((N_ROW,)),
             dma((N_ROW,)),
             dma((N_COL,)),

time: 64.8 us -> 62.4 us (0.963)
  Pallas kernels: 63.6 us -> 61.3 us
    pallas_call x1, Pallas kernels: 59.7 us -> 57.4 us  [body(): pl.pallas_call(kernel, out_shape=(pltpu.VMEM((N_COL, N_ROW, R, R), jnp.fl...]
where the time goes in v5:
time: 62.4 us; the launch traced here: 62 us
  Pallas kernels  61.3 us (98%)
  between operations  0.66 us (1%)
    pallas_call x1, Pallas kernels, body(): pl.pallas_call(kernel, out_shape=(pltpu.VMEM((N_COL, N_ROW, R, R), jnp.fl...  57.4 us
    pallas_call x1, Pallas kernels, body(): pl.pallas_call(finish, out_shape=(jax.ShapeDtypeStruct(out.shape, jnp.flo...  3.91 us

profile of v5, /device:TPU:1, one launch (start us, length us, event | category | flops | bytes accessed | tf_op | source)
XLA Modules:
  0.0 62.0 jit_solution(11886466530763109193)
XLA Ops:
  0.7 57.4 %shard_map.55 = (f32[16,8,128,128]{3,2,1,0:T(8,128)S(1)}, bf16[8,1536,128]{2,1,0:T(8,128)(2,1)S(1)}, bf16[16,128,1536]{2,1,0:T(8,128)(2,1)S(1)}) custom-call(s32[128]{0:T(128)} %owner_hbm.1, s32[1]{0:T(128)S(6)} %copy.8.rank_hbm, bf16[16,96,128]{2,1,0:T(8,128)(2,1)} %panel_hbm.1, bf16[1536,1536]{1,0:T(8,128)(2,1)} %inverse_hbm.1, f32[16,8,128,128]{3,2,1,0:T(8,128)} %bitcast.2), custom_call_target="tpu_custom_call" | custom-call | flops 6442450944 | bytes 16777216 | tf_op jit(solution)/shard_map/pallas_call | solution.py:335
  58.1 3.9 %shard_map.56 = (f32[16,8,128,128]{3,2,1,0:T(8,128)}, f32[16,8,128,128]{3,2,1,0:T(8,128)S(1)}) custom-call(bf16[16,128,1536]{2,1,0:T(8,128)(2,1)S(1)} %get-tuple-element.9.left, bf16[8,1536,128]{2,1,0:T(8,128)(2,1)S(1)} %get-tuple-element.10.right, f32[16,8,128,128]{3,2,1,0:T(8,128)S(1)} %get-tuple-element.11.grams_in), custom_call_target="tpu_custom_call", output_to_operand_aliasing={{1}: (2, {})} | custom-call | tf_op jit(solution)/shard_map/pallas_call | solution.py:372

commit v6 on v5

--- a/solution.py
+++ b/solution.py
@@ -40,7 +40,8 @@
     (GRAM, 0, 0, 2), (GRAM, 2, 0, 2), (FAR, LEFT, 1), (SHARE, 2, 1),
     (GRAM, 3, 0, 0), (GRAM, 1, 0, 2), (GRAM, 2, 0, 1), (GRAM, 3, 0, 2),
     (WAIT, 3, 1), (WAIT, 1, 1), (GRAM, 1, 1, 1), (GRAM, 1, 1, 0),
-    (GRAM, 3, 1, 1), (GRAM, 3, 1, 0), (FAR, RIGHT, 1), (WAIT, 2, 1),
+    (GRAM, 3, 1, 1), (GRAM, 3, 1, 0), (GRAM, 1, 1, 2), (GRAM, 3, 1, 2),
+    (FAR, RIGHT, 1), (WAIT, 2, 1),
 )
 
 
@@ -97,6 +98,9 @@
     x, zh = r // 2, r % 2
     y, zl, h = c // 4, (c // 2) % 2, c % 2
 
+    panel_copy = pltpu.make_async_copy(panel_hbm, panel, local_sem.at[3])
+    panel_copy.start()
+
     barrier = pltpu.get_barrier_semaphore()
     for d in range(1, N_ROW):
         pl.semaphore_signal(barrier, inc=1, device_id={"row": (r + d) % N_ROW, "col": c}, device_id_type=MESH)
@@ -104,10 +108,9 @@
         pl.semaphore_signal(barrier, inc=1, device_id={"row": r, "col": (c + d) % N_COL}, device_id_type=MESH)
     inverse_copy = pltpu.make_async_copy(inverse_hbm, inverse, local_sem.at[0])
     cores_copy = pltpu.make_async_copy(cores_hbm, out_ref, local_sem.at[1])
-    panel_copy = pltpu.make_async_copy(panel_hbm, panel, local_sem.at[3])
     rank_copy = pltpu.make_async_copy(rank_hbm, rank_ref, local_sem.at[4])
     owner_copy = pltpu.make_async_copy(owner_hbm, owner_ref, local_sem.at[5])
-    for copy in (panel_copy, rank_copy, owner_copy):
+    for copy in (rank_copy, owner_copy):
         copy.start()
     panel_copy.wait()
     pl.semaphore_wait(barrier, N_ROW + N_COL - 2)
@@ -211,9 +214,7 @@
         rows = slice(i * step, (i + 1) * step)
         done = (i + 1) * step
         solved = jnp.dot(inverse[rows, :done], held[:done, :], preferred_element_type=jnp.float32)
-        solved = jnp.where(keep, solved, 0.0)
-        right[r, rows, :] = solved.astype(jnp.bfloat16)
-        left[c, :, rows] = solved.T.astype(jnp.bfloat16)
+        right[r, rows, :] = jnp.where(keep, solved, 0.0).astype(jnp.bfloat16)
 
     def row_of(dx, flip):
         return ((x + dx) % 4) * 2 + (1 - zh if flip else zh)
@@ -258,10 +259,15 @@
                 send_left(c, part, 0, 1)
         del z_order[:count]
 
+    for step in range(CUTS):
+        for first, d in ((0, 1), (2, -1)):
+            send_right(r, (first + step) % CUTS, d)
+    for i in range(B // 256):
+        rows = slice(i * 256, (i + 1) * 256)
+        left[c, :, rows] = right[r, rows, :].astype(jnp.float32).T.astype(jnp.bfloat16)
     along_z(2)
     for step in range(CUTS):
         for first, d in ((0, 1), (2, -1)):
-            send_right(r, (first + step) % CUTS, d)
             send_left(c, (first + step) % CUTS, d)
         if step:
             along_z(2)

time: 62.4 us -> 62.5 us (level)
  no operation moved by 1% of the time
where the time goes in v6:
time: 62.5 us; the launch traced here: 62.3 us
  Pallas kernels  61.7 us (99%)
  between operations  0.66 us (1%)
    pallas_call x1, Pallas kernels, body(): pl.pallas_call(kernel, out_shape=(pltpu.VMEM((N_COL, N_ROW, R, R), jnp.fl...  57.9 us
    pallas_call x1, Pallas kernels, body(): pl.pallas_call(finish, out_shape=(jax.ShapeDtypeStruct(out.shape, jnp.flo...  3.83 us

profile of v6, /device:TPU:1, one launch (start us, length us, event | category | flops | bytes accessed | tf_op | source)
XLA Modules:
  0.0 62.3 jit_solution(4243884962391633155)
XLA Ops:
  0.7 57.9 %shard_map.55 = (f32[16,8,128,128]{3,2,1,0:T(8,128)S(1)}, bf16[8,1536,128]{2,1,0:T(8,128)(2,1)S(1)}, bf16[16,128,1536]{2,1,0:T(8,128)(2,1)S(1)}) custom-call(s32[128]{0:T(128)} %owner_hbm.1, s32[1]{0:T(128)S(6)} %copy.8.rank_hbm, bf16[16,96,128]{2,1,0:T(8,128)(2,1)} %panel_hbm.1, bf16[1536,1536]{1,0:T(8,128)(2,1)} %inverse_hbm.1, f32[16,8,128,128]{3,2,1,0:T(8,128)} %bitcast.2), custom_call_target="tpu_custom_call" | custom-call | flops 6442450944 | bytes 16777216 | tf_op jit(solution)/shard_map/pallas_call | solution.py:341
  58.5 3.8 %shard_map.56 = (f32[16,8,128,128]{3,2,1,0:T(8,128)}, f32[16,8,128,128]{3,2,1,0:T(8,128)S(1)}) custom-call(bf16[16,128,1536]{2,1,0:T(8,128)(2,1)S(1)} %get-tuple-element.9.left, bf16[8,1536,128]{2,1,0:T(8,128)(2,1)S(1)} %get-tuple-element.10.right, f32[16,8,128,128]{3,2,1,0:T(8,128)S(1)} %get-tuple-element.11.grams_in), custom_call_target="tpu_custom_call", output_to_operand_aliasing={{1}: (2, {})} | custom-call | tf_op jit(solution)/shard_map/pallas_call | solution.py:378

commit v7 on v6

--- a/solution.py
+++ b/solution.py
@@ -37,7 +37,7 @@
     (GRAM, 0, 0, 1), (NEAR, LEFT, 1, 1, 3), (GRAM, 2, 0, 0), (NEAR, LEFT, 1, -1, 3),
     (SHARE, 1, 1), (SHARE, 3, 1), (NEAR, RIGHT, 1, -1, 3), (NEAR, RIGHT, 1, 1, 3),
     (NEAR, RIGHT, 1, 1, 1), (GRAM, 1, 0, 1), (GRAM, 0, 1, 2), (GRAM, 0, 1, 1),
-    (GRAM, 0, 0, 2), (GRAM, 2, 0, 2), (FAR, LEFT, 1), (SHARE, 2, 1),
+    (GRAM, 0, 0, 2), (GRAM, 2, 0, 2), (FAR, LEFT, 1),
     (GRAM, 3, 0, 0), (GRAM, 1, 0, 2), (GRAM, 2, 0, 1), (GRAM, 3, 0, 2),
     (WAIT, 3, 1), (WAIT, 1, 1), (GRAM, 1, 1, 1), (GRAM, 1, 1, 0),
     (GRAM, 3, 1, 1), (GRAM, 3, 1, 0), (GRAM, 1, 1, 2), (GRAM, 3, 1, 2),
@@ -98,9 +98,6 @@
     x, zh = r // 2, r % 2
     y, zl, h = c // 4, (c // 2) % 2, c % 2
 
-    panel_copy = pltpu.make_async_copy(panel_hbm, panel, local_sem.at[3])
-    panel_copy.start()
-
     barrier = pltpu.get_barrier_semaphore()
     for d in range(1, N_ROW):
         pl.semaphore_signal(barrier, inc=1, device_id={"row": (r + d) % N_ROW, "col": c}, device_id_type=MESH)
@@ -108,9 +105,10 @@
         pl.semaphore_signal(barrier, inc=1, device_id={"row": r, "col": (c + d) % N_COL}, device_id_type=MESH)
     inverse_copy = pltpu.make_async_copy(inverse_hbm, inverse, local_sem.at[0])
     cores_copy = pltpu.make_async_copy(cores_hbm, out_ref, local_sem.at[1])
+    panel_copy = pltpu.make_async_copy(panel_hbm, panel, local_sem.at[3])
     rank_copy = pltpu.make_async_copy(rank_hbm, rank_ref, local_sem.at[4])
     owner_copy = pltpu.make_async_copy(owner_hbm, owner_ref, local_sem.at[5])
-    for copy in (rank_copy, owner_copy):
+    for copy in (panel_copy, rank_copy, owner_copy):
         copy.start()
     panel_copy.wait()
     pl.semaphore_wait(barrier, N_ROW + N_COL - 2)
@@ -173,7 +171,7 @@
     def _():
         @pl.loop(1, NP)
         def _(d):
-            p = (me + d) % NP
+            p = (r + d) % N_ROW * N_COL + (c + d // N_ROW) % N_COL
             moved[p] = spread[owner_ref[p]]
             pltpu.make_async_remote_copy(
                 src_ref=moved.at[p], dst_ref=held.at[own_rows, :],
@@ -302,13 +300,20 @@
             send_left(col_of(2, 0), rest[0], 0, 1)
         elif step == FAR:
             kind, flip = rest
-            for part in range(CUTS):
+            for part in (1, 3, 0, 2):
                 if kind == RIGHT:
                     wait_right(row_of(2, flip), part)
-                elif flip or part % 2 == 0:
-                    wait_left(col_of(2, flip), part)
+                elif flip:
+                    wait_left(col_of(2, 1), part)
+                    ref = half(left, col_of(2, 1), part)
+                    send(ref, ref, sem_left.at[col_of(2, 1), part], r, sibling, TO_COL)
+                elif part % 2 == 0:
+                    wait_left(col_of(2, 0), part)
         elif step == SHARE:
             share(col_of(*rest))
+        elif step == WAIT and rest == [2, 1]:
+            for part in range(CUTS):
+                wait_left(col_of(2, 1, 1), part)
         elif step == WAIT:
             wait_shared(col_of(*rest, 1))
         else:

time: 62.5 us -> 62.5 us (level)
  no operation moved by 1% of the time
where the time goes in v7:
time: 62.5 us; the launch traced here: 62.4 us
  Pallas kernels  61.7 us (99%)
  between operations  0.66 us (1%)
    pallas_call x1, Pallas kernels, body(): pl.pallas_call(kernel, out_shape=(pltpu.VMEM((N_COL, N_ROW, R, R), jnp.fl...  57.9 us
    pallas_call x1, Pallas kernels, body(): pl.pallas_call(finish, out_shape=(jax.ShapeDtypeStruct(out.shape, jnp.flo...  3.83 us

profile of v7, /device:TPU:1, one launch (start us, length us, event | category | flops | bytes accessed | tf_op | source)
XLA Modules:
  0.0 62.4 jit_solution(16442376192382951274)
XLA Ops:
  0.7 57.9 %shard_map.55 = (f32[16,8,128,128]{3,2,1,0:T(8,128)S(1)}, bf16[8,1536,128]{2,1,0:T(8,128)(2,1)S(1)}, bf16[16,128,1536]{2,1,0:T(8,128)(2,1)S(1)}) custom-call(s32[128]{0:T(128)} %owner_hbm.1, s32[1]{0:T(128)S(6)} %copy.8.rank_hbm, bf16[16,96,128]{2,1,0:T(8,128)(2,1)} %panel_hbm.1, bf16[1536,1536]{1,0:T(8,128)(2,1)} %inverse_hbm.1, f32[16,8,128,128]{3,2,1,0:T(8,128)} %bitcast.2), custom_call_target="tpu_custom_call" | custom-call | flops 6442450944 | bytes 16777216 | tf_op jit(solution)/shard_map/pallas_call | solution.py:346
  58.6 3.8 %shard_map.56 = (f32[16,8,128,128]{3,2,1,0:T(8,128)}, f32[16,8,128,128]{3,2,1,0:T(8,128)S(1)}) custom-call(bf16[16,128,1536]{2,1,0:T(8,128)(2,1)S(1)} %get-tuple-element.9.left, bf16[8,1536,128]{2,1,0:T(8,128)(2,1)S(1)} %get-tuple-element.10.right, f32[16,8,128,128]{3,2,1,0:T(8,128)S(1)} %get-tuple-element.11.grams_in), custom_call_target="tpu_custom_call", output_to_operand_aliasing={{1}: (2, {})} | custom-call | tf_op jit(solution)/shard_map/pallas_call | solution.py:383
